TPU v7x, 256 devices: a whole 4x4x8 slice. The times are simulated.
256 devices in a mesh: col: 16 (over x, y), row: 8 (over z), pair: 2 (over core).
Axes of the slice: x: 4, y: 4, z: 8, core: 2. Of those that a mesh axis runs over, the one named last changes fastest.
Arguments:
- tokens: bfloat16 [2, 8192, 2880], P(None, ('col', 'row')), may hold values from -6 to 6
- expert_ids: int32 [2, 8192, 4], P(None, ('col', 'row')), may hold values from 0 to 127, all different within a row; in each aligned block of 64 rows (0 to 63, 64 to 127, ..., all dimensions but the last counted through in order) at most 3 rows name the same one
- gate_weights: float32 [2, 8192, 4], P(None, ('col', 'row')), may hold values from 0.05 to 0.6
- migration: int32 [32, 2], replicated, may hold values from 0 to 127, as said below
- up_values: bfloat16 [128, 2880, 1536], P(('col', 'row'), None, 'pair'), may hold values from -0.109375 to 0.109375
- up_scales: bfloat16 [128, 90, 1536], P(('col', 'row'), None, 'pair'), may hold values from 0.3984375 to 2.5
- down_values: bfloat16 [128, 1536, 2880], P(('col', 'row'), 'pair'), may hold values from -0.15625 to 0.15625
- down_scales: bfloat16 [128, 48, 2880], P(('col', 'row'), 'pair'), may hold values from 0.3984375 to 2.5
Outputs:
- mixed: bfloat16 [2, 8192, 2880], P(None, ('col', 'row'), 'pair')
Inputs may be any that keep to these rules, and one draw needn't show every extreme that they name: `expert_ids`: each token names 4 different experts. Among one group's 64 tokens of one batch (an aligned block of rows), no expert is named more than 3 times, a bound that some block reaches. `migration`: column 0 names 32 different experts; column 1 names the same experts in another order, none in its own row's place.
All inputs are finite; a program needn't handle non-finite values.
Results may differ from a plain program's by a relative error of at most 0.0077.
Values may be sent and summed in bfloat16 or wider, within the bound.
No kernel may reach another device: no remote copies, remote signals or barrier semaphores. Data moves between devices by JAX's collectives and lax.ppermute only.
A program may use at most 128 MiB of HBM per device.

v0:
```python
import jax
import jax.numpy as jnp
from jax import lax
from jax.sharding import PartitionSpec as P

TOP = 4


def in_blocks(x, dim, peers):
    lengths = x.shape
    blocks = x.reshape(*lengths[:dim], peers, lengths[dim] // peers, *lengths[dim + 1 :])
    return jnp.moveaxis(blocks, dim, 0)


def laid_out(blocks, dim):
    lengths = list(blocks.shape[1:])
    lengths[dim] *= blocks.shape[0]
    return jnp.moveaxis(blocks, 0, dim).reshape(lengths)


def joined_exchange(x, axis, axes, splits, concats):
    sizes = [lax.axis_size(a) for a in axes]
    blocks = in_blocks(x, splits[0], sizes[0])
    blocks = jnp.moveaxis(in_blocks(blocks, splits[1] + 1, sizes[1]), 0, 1)
    inside = blocks.shape[2:]
    blocks = blocks.reshape(-1, *inside)
    blocks = lax.all_to_all(blocks, axis, split_axis=0, concat_axis=0, tiled=True)
    blocks = laid_out(blocks.reshape(*sizes, *inside), concats[0] + 1)
    return laid_out(blocks, concats[1])


def sent_and_summed(x, axis, dim):
    blocks = in_blocks(x, dim, lax.axis_size(axis))
    arrived = lax.all_to_all(blocks, axis, split_axis=0, concat_axis=0, tiled=True)
    return arrived.astype(jnp.float32).sum(axis=0)


def dequantize(values, scales):
    blocks = scales.shape[0]
    cols = values.shape[1]
    shaped = values.reshape(blocks, 32, cols).astype(jnp.float32)
    product = shaped * scales.astype(jnp.float32)[:, None, :]
    return product.reshape(blocks * 32, cols).astype(jnp.bfloat16)


def activate(pre_act):
    return pre_act * jax.nn.sigmoid(1.702 * pre_act)


def source_table(migration, experts):
    slot_ids = jnp.arange(experts, dtype=jnp.int32)
    matches = (migration[None, :, 1] == slot_ids[:, None]).astype(jnp.int32)
    return slot_ids + jnp.sum(matches * (migration[None, :, 0] - slot_ids[:, None]), axis=1)


def relabel(ids_now, sources):
    slot_ids = jnp.arange(sources.shape[0], dtype=jnp.int32)
    matches = (ids_now[..., None] == slot_ids).astype(jnp.int32)
    return jnp.sum(matches * sources, axis=-1)


def pack_slots(tokens_now, ids_now, experts, capacity):
    tok_rows = tokens_now.shape[0]
    flat_ids = ids_now.reshape(-1)
    onehot = (flat_ids[:, None] == jnp.arange(experts, dtype=jnp.int32)[None, :]).astype(jnp.int32)
    before = jnp.cumsum(onehot, axis=0) - onehot
    slot_index = jnp.sum(before * onehot, axis=1)
    position = flat_ids * capacity + slot_index
    select = (jnp.arange(experts * capacity, dtype=jnp.int32)[:, None] == position[None, :]).astype(
        jnp.int32
    )
    select = jnp.sum(select.reshape(experts * capacity, tok_rows, TOP), axis=2).astype(jnp.bfloat16)
    packed = jnp.dot(select, tokens_now, preferred_element_type=jnp.float32).astype(jnp.bfloat16)
    return (packed.reshape(experts, capacity, tokens_now.shape[1]), position)


def send_out(packed):
    col_count = lax.axis_size("col")
    grid_view = packed.reshape((col_count, packed.shape[0] // col_count) + packed.shape[1:])
    moved_grid = joined_exchange(grid_view, ("col", "row"), ("col", "row"), (0, 1), (0, 1))
    return moved_grid.reshape(packed.shape)


def send_back(results):
    col_count = lax.axis_size("col")
    grid_view = results.reshape((col_count, results.shape[0] // col_count) + results.shape[1:])
    moved_grid = joined_exchange(grid_view, ("col", "row"), ("col", "row"), (0, 1), (0, 1))
    return moved_grid.reshape(results.shape)


def expert_rows(received, up_weight, down_weight):
    flat_rows = received.reshape(-1, received.shape[-1])
    pre_act = jnp.dot(flat_rows, up_weight, preferred_element_type=jnp.float32)
    hidden = activate(pre_act).astype(jnp.bfloat16)
    partial_value = jnp.dot(hidden, down_weight, preferred_element_type=jnp.float32).astype(
        jnp.bfloat16
    )
    partial_value = lax.optimization_barrier(partial_value).astype(jnp.float32)
    summed = sent_and_summed(partial_value.reshape(received.shape).astype(jnp.bfloat16), "pair", 2)
    return summed.astype(jnp.bfloat16)


def combine(returned, position, gates_now):
    flat_rows = returned.reshape(-1, returned.shape[-1])
    picked = jnp.take(flat_rows, position, axis=0).astype(jnp.float32)
    picked = picked.reshape(gates_now.shape + (flat_rows.shape[-1],))
    return jnp.sum(gates_now[..., None] * picked, axis=1).astype(jnp.bfloat16)


def run_batch(tokens_now, ids_now, gates_now, up_weight, down_weight, experts, capacity):
    packed, position = pack_slots(tokens_now, ids_now, experts, capacity)
    received = send_out(packed)
    returned = send_back(expert_rows(received, up_weight, down_weight))
    return combine(returned, position, gates_now)


def per_device(
    tokens, expert_ids, gate_weights, migration, up_values, up_scales, down_values, down_scales
):
    experts = lax.axis_size("col") * lax.axis_size("row")
    capacity = max(2, 3 * tokens.shape[1] * TOP // (2 * experts))
    sources = source_table(migration, experts)
    up_weight = dequantize(up_values[0], up_scales[0])
    down_weight = dequantize(down_values[0], down_scales[0])
    first_out = run_batch(
        tokens[0], expert_ids[0], gate_weights[0], up_weight, down_weight, experts, capacity
    )
    second = run_batch(
        tokens[1],
        relabel(expert_ids[1], sources),
        gate_weights[1],
        up_weight,
        down_weight,
        experts,
        capacity,
    )
    return jnp.stack([first_out, second], axis=0)


def solution(mesh):
    placed = (
        P(None, ("col", "row"), None),
        P(None, ("col", "row"), None),
        P(None, ("col", "row"), None),
        P(),
        P(("col", "row"), None, "pair"),
        P(("col", "row"), None, "pair"),
        P(("col", "row"), "pair", None),
        P(("col", "row"), "pair", None),
    )
    return jax.shard_map(
        per_device,
        mesh=mesh,
        in_specs=placed,
        out_specs=P(None, ("col", "row"), "pair"),
        check_vma=False,
    )
```

profile of v0, /device:TPU:1, one launch (start us, length us, event | category | flops | bytes accessed | tf_op | source)
XLA Modules:
  0.0 361.2 jit_solution(10481464912024519141)
XLA Ops:
  7.4 5.8 %reshape_transpose_transpose_reshape_reshape_reshape_reshape.7 = bf16[128,1,1,3,2880]{4,3,0,2,1:T(4,128)(2,1)} reshape(bf16[384,2880]{1,0:T(8,128)(2,1)} %copy.80) | data formatting | bytes 4423680 | tf_op jit(solution)/shard_map/reshape;transpose;transpose;reshape;reshape;reshape;reshape | solution.py:26
  13.2 16.8 %all-to-all-start.3 = ((bf16[128,1,1,3,2880]{4,3,2,1,0:T(4,128)(2,1)}), bf16[128,1,1,3,2880]{4,3,2,1,0:T(4,128)(2,1)S(1)}, u32[]{:S(2)}, u32[]{:S(2)}) async-start(bf16[128,1,1,3,2880]{4,3,2,1,0:T(4,128)(2,1)} %bitcast.113), calls=%async_computation.3 | async-start | bytes 6029312 | tf_op jit(solution)/shard_map/all_to_all | solution.py:27
  30.3 6.5 %copy.70 = bf16[1,768,2880]{2,1,0:T(8,128)(2,1)} copy(bf16[1,768,2880]{1,2,0:T(8,128)(2,1)} %param.16) | data formatting | bytes 8847360 | tf_op args[6]
  40.9 4.2 %copy.68 = bf16[384,2880]{1,0:T(8,128)(2,1)} copy(bf16[384,2880]{0,1:T(8,128)(2,1)} %convolution_convert_fusion.3) | data formatting | bytes 4423680 | tf_op jit(solution)/shard_map/convert_element_type | solution.py:73
  45.1 5.8 %reshape_transpose_transpose_reshape_reshape_reshape_reshape.6 = bf16[128,1,1,3,2880]{4,3,0,2,1:T(4,128)(2,1)} reshape(bf16[384,2880]{1,0:T(8,128)(2,1)} %copy.68) | data formatting | bytes 4423680 | tf_op jit(solution)/shard_map/reshape;transpose;transpose;reshape;reshape;reshape;reshape | solution.py:26
  51.0 5.3 %fusion = bf16[768,2880]{1,0:T(8,128)(2,1)} fusion(bf16[1,768,2880]{2,1,0:T(8,128)(2,1)} %copy.70, f32[24,2880]{1,0:T(8,128)S(1)} %bitcast_convert_fusion.1), kind=kLoop, calls=%fused_computation.3 | loop fusion | flops 6635520 | bytes 9123840 | tf_op jit(solution)/shard_map/convert_element_type | solution.py:43
  56.4 3.6 fusion.1
  60.0 42.2 %all-to-all-done.3 = bf16[128,1,1,3,2880]{4,3,2,1,0:T(4,128)(2,1)S(1)} async-done(((bf16[128,1,1,3,2880]{4,3,2,1,0:T(4,128)(2,1)}), bf16[128,1,1,3,2880]{4,3,2,1,0:T(4,128)(2,1)S(1)}, u32[]{:S(2)}, u32[]{:S(2)}) %all-to-all-start.3) | async-done | bytes 2211872 | tf_op jit(solution)/shard_map/all_to_all | solution.py:27
  105.2 8.8 %convolution_convert_fusion = bf16[384,2880]{0,1:T(8,128)(2,1)S(1)} fusion(bf16[768,2880]{1,0:T(8,128)(2,1)} %fusion, bf16[384,2880]{1,0:T(8,128)(2,1)} %reshape_reshape_reshape.14, bf16[2880,768]{1,0:T(8,128)(2,1)} %bitcast.120), kind=kOutput, calls=%fused_computation.6 | convolution fusion | flops 3400261632 | bytes 13271040 | tf_op jit(solution)/shard_map/dot_general | solution.py:95
  116.6 6.9 %convert_element_type.184 = bf16[128,3,2,1440]{3,2,1,0:T(2,128)(2,1)S(1)} reshape(bf16[384,2880]{1,0:T(8,128)(2,1)} %copy.82) | data formatting | bytes 4423680 | tf_op jit(solution)/shard_map/convert_element_type | solution.py:99
  123.4 4.6 %copy.83 = bf16[2,128,3,1440]{1,3,2,0:T(8,128)(2,1)} copy(bf16[2,128,3,1440]{3,0,2,1:T(2,128)(2,1)S(1)} %bitcast.115) | data formatting | bytes 4423680 | tf_op jit(solution)/shard_map/transpose | solution.py:12
  128.1 11.4 %all_to_all.30 = bf16[2,128,3,1440]{1,3,2,0:T(8,128)(2,1)} all-to-all(bf16[2,128,3,1440]{1,3,2,0:T(8,128)(2,1)} %copy.83), channel_id=1, replica_groups=mesh['col'=16,'row'=8,'pair'=2] {'pair'}, dimensions={0} | all-to-all | bytes 4423680 | tf_op jit(solution)/shard_map/all_to_all | solution.py:34
  139.5 6.2 %all-to-all-start = ((bf16[128,1,1,3,2880]{4,3,2,1,0:T(4,128)(2,1)}), bf16[128,1,1,3,2880]{4,3,2,1,0:T(4,128)(2,1)S(1)}, u32[]{:S(2)}, u32[]{:S(2)}) async-start(bf16[128,1,1,3,2880]{4,3,2,1,0:T(4,128)(2,1)} %bitcast.6), calls=%async_computation | async-start | bytes 6029312 | tf_op jit(solution)/shard_map/all_to_all | solution.py:27
  145.7 3.3 reduce_sum.110
  149.0 3.8 %copy.84 = bf16[128,1,1,3,1440]{4,3,2,1,0:T(4,128)(2,1)} copy(bf16[128,1,1,3,1440]{0,4,3,2,1:T(8,128)(2,1)} %bitcast.123) | data formatting | bytes 2211840 | tf_op jit(solution)/shard_map/reshape;transpose;transpose;reshape;reshape;reshape | solution.py:26
  152.9 65.1 %all-to-all-done = bf16[128,1,1,3,2880]{4,3,2,1,0:T(4,128)(2,1)S(1)} async-done(((bf16[128,1,1,3,2880]{4,3,2,1,0:T(4,128)(2,1)}), bf16[128,1,1,3,2880]{4,3,2,1,0:T(4,128)(2,1)S(1)}, u32[]{:S(2)}, u32[]{:S(2)}) %all-to-all-start) | async-done | bytes 2211872 | tf_op jit(solution)/shard_map/all_to_all | solution.py:27
  221.1 8.8 %convolution_convert_fusion.2 = bf16[384,2880]{0,1:T(8,128)(2,1)S(1)} fusion(bf16[768,2880]{1,0:T(8,128)(2,1)} %fusion, bf16[384,2880]{1,0:T(8,128)(2,1)} %reshape_reshape_reshape.12, bf16[2880,768]{1,0:T(8,128)(2,1)} %bitcast.121), kind=kOutput, calls=%fused_computation.8 | convolution fusion | flops 3400261632 | bytes 13271040 | tf_op jit(solution)/shard_map/dot_general | solution.py:95
  232.4 6.9 %convert_element_type.174 = bf16[128,3,2,1440]{3,2,1,0:T(2,128)(2,1)S(1)} reshape(bf16[384,2880]{1,0:T(8,128)(2,1)} %copy.71) | data formatting | bytes 4423680 | tf_op jit(solution)/shard_map/convert_element_type | solution.py:99
  239.3 4.6 %copy.72 = bf16[2,128,3,1440]{1,3,2,0:T(8,128)(2,1)} copy(bf16[2,128,3,1440]{3,0,2,1:T(2,128)(2,1)S(1)} %bitcast.116) | data formatting | bytes 4423680 | tf_op jit(solution)/shard_map/transpose | solution.py:12
  243.9 9.1 %all_to_all.31 = bf16[2,128,3,1440]{1,3,2,0:T(8,128)(2,1)S(1)} all-to-all(bf16[2,128,3,1440]{1,3,2,0:T(8,128)(2,1)} %copy.72), channel_id=1, replica_groups=mesh['col'=16,'row'=8,'pair'=2] {'pair'}, dimensions={0} | all-to-all | bytes 4423680 | tf_op jit(solution)/shard_map/all_to_all | solution.py:34
  253.0 7.5 %all-to-all-start.5 = ((bf16[128,1,1,3,1440]{4,3,2,1,0:T(4,128)(2,1)}), bf16[128,1,1,3,1440]{4,3,2,1,0:T(4,128)(2,1)}, u32[]{:S(2)}, u32[]{:S(2)}) async-start(bf16[128,1,1,3,1440]{4,3,2,1,0:T(4,128)(2,1)} %copy.84), calls=%async_computation.5 | async-start | bytes 3145728 | tf_op jit(solution)/shard_map/all_to_all | solution.py:27
  264.5 37.7 %all-to-all-done.5 = bf16[128,1,1,3,1440]{4,3,2,1,0:T(4,128)(2,1)} async-done(((bf16[128,1,1,3,1440]{4,3,2,1,0:T(4,128)(2,1)}), bf16[128,1,1,3,1440]{4,3,2,1,0:T(4,128)(2,1)}, u32[]{:S(2)}, u32[]{:S(2)}) %all-to-all-start.5) | async-done | bytes 1105952 | tf_op jit(solution)/shard_map/all_to_all | solution.py:27
  302.2 7.3 %all-to-all-start.2 = ((bf16[128,1,1,3,1440]{4,3,2,1,0:T(4,128)(2,1)}), bf16[128,1,1,3,1440]{4,3,2,1,0:T(4,128)(2,1)}, u32[]{:S(2)}, u32[]{:S(2)}) async-start(bf16[128,1,1,3,1440]{4,3,2,1,0:T(4,128)(2,1)} %copy.73), calls=%async_computation.2 | async-start | bytes 3145728 | tf_op jit(solution)/shard_map/all_to_all | solution.py:27
  318.1 31.3 %all-to-all-done.2 = bf16[128,1,1,3,1440]{4,3,2,1,0:T(4,128)(2,1)} async-done(((bf16[128,1,1,3,1440]{4,3,2,1,0:T(4,128)(2,1)}), bf16[128,1,1,3,1440]{4,3,2,1,0:T(4,128)(2,1)}, u32[]{:S(2)}, u32[]{:S(2)}) %all-to-all-start.2) | async-done | bytes 1105952 | tf_op jit(solution)/shard_map/all_to_all | solution.py:27
  (83 shorter events, 47.2 us)
Async XLA Ops:
  13.2 89.0 %all-to-all-start.3 = ((bf16[128,1,1,3,2880]{4,3,2,1,0:T(4,128)(2,1)}), bf16[128,1,1,3,2880]{4,3,2,1,0:T(4,128)(2,1)S(1)}, u32[]{:S(2)}, u32[]{:S(2)}) async-start(bf16[128,1,1,3,2880]{4,3,2,1,0:T(4,128)(2,1)} %bitcast.113), calls=%async_computation.3 | async-start | bytes 6029312 | tf_op jit(solution)/shard_map/all_to_all | solution.py:27
  45.1 5.8 %copy-start.2 = (bf16[1,24,2880]{2,1,0:T(8,128)(2,1)S(1)}, bf16[1,24,2880]{2,1,0:T(8,128)(2,1)}, u32[]{:S(2)}) copy-start(bf16[1,24,2880]{2,1,0:T(8,128)(2,1)} %param.17) | copy-start | bytes 414724
  51.0 5.4 %slice-start = ((s8[4423680]{0:T(1024)(128)(4,1)}), s8[4194304]{0:T(1024)(128)(4,1)S(1)}, s32[]{:S(2)}) async-start(s8[4423680]{0:T(1024)(128)(4,1)} %bitcast.117), calls=%async_computation.6 | async-start | bytes 8388608
  51.0 5.4 %copy-start.1 = (bf16[1,90,768]{2,1,0:T(8,128)(2,1)S(1)}, bf16[1,90,768]{2,1,0:T(8,128)(2,1)}, u32[]{:S(2)}) copy-start(bf16[1,90,768]{2,1,0:T(8,128)(2,1)} %param.15) | copy-start | bytes 414724
  51.0 5.4 %slice-start.1 = ((s8[4423680]{0:T(1024)(128)(4,1)}), s8[229376]{0:T(1024)(128)(4,1)S(1)}, s32[]{:S(2)}) async-start(s8[4423680]{0:T(1024)(128)(4,1)} %bitcast.117), calls=%async_computation.7 | async-start | bytes 458752
  139.5 78.5 %all-to-all-start = ((bf16[128,1,1,3,2880]{4,3,2,1,0:T(4,128)(2,1)}), bf16[128,1,1,3,2880]{4,3,2,1,0:T(4,128)(2,1)S(1)}, u32[]{:S(2)}, u32[]{:S(2)}) async-start(bf16[128,1,1,3,2880]{4,3,2,1,0:T(4,128)(2,1)} %bitcast.6), calls=%async_computation | async-start | bytes 6029312 | tf_op jit(solution)/shard_map/all_to_all | solution.py:27
  253.0 49.2 %all-to-all-start.5 = ((bf16[128,1,1,3,1440]{4,3,2,1,0:T(4,128)(2,1)}), bf16[128,1,1,3,1440]{4,3,2,1,0:T(4,128)(2,1)}, u32[]{:S(2)}, u32[]{:S(2)}) async-start(bf16[128,1,1,3,1440]{4,3,2,1,0:T(4,128)(2,1)} %copy.84), calls=%async_computation.5 | async-start | bytes 3145728 | tf_op jit(solution)/shard_map/all_to_all | solution.py:27
  261.6 47.9 %copy-start.5 = (f32[2,64,4]{1,2,0:T(4,128)S(1)}, f32[2,64,4]{1,2,0:T(4,128)}, u32[]{:S(2)}) copy-start(f32[2,64,4]{1,2,0:T(4,128)} %param.12) | copy-start | bytes 6148
  302.2 47.3 %all-to-all-start.2 = ((bf16[128,1,1,3,1440]{4,3,2,1,0:T(4,128)(2,1)}), bf16[128,1,1,3,1440]{4,3,2,1,0:T(4,128)(2,1)}, u32[]{:S(2)}, u32[]{:S(2)}) async-start(bf16[128,1,1,3,1440]{4,3,2,1,0:T(4,128)(2,1)} %copy.73), calls=%async_computation.2 | async-start | bytes 3145728 | tf_op jit(solution)/shard_map/all_to_all | solution.py:27
  353.6 4.1 %copy-start.3 = (f32[64,4]{1,0:T(8,128)S(1)}, f32[64,4]{1,0:T(8,128)}, u32[]{:S(2)}) copy-start(f32[64,4]{1,0:T(8,128)} %copy.74) | copy-start | bytes 3076
  354.9 3.9 %copy-start.4 = (f32[64,4]{1,0:T(8,128)S(1)}, f32[64,4]{1,0:T(8,128)}, u32[]{:S(2)}) copy-start(f32[64,4]{1,0:T(8,128)} %copy.63) | copy-start | bytes 3076
  357.7 1.4 copy-start
where the time goes:
time: 367 us; the launch traced here: 361 us
  waiting for transfers between devices  176 us (48%)
  local copies, waits for them, and re-layouts  83 us (23%)
  starting transfers between devices  37.7 us (10%)
  matrix products  22.5 us (6%)
  other arithmetic  20.5 us (6%)
  blocking collectives  20.5 us (6%)
    all_to_all x4, waiting for transfers between devices, joined_exchange(): lax.all_to_all(blocks, axis, split_axis=0, concat_axis=0, tiled=True)  176 us
    all_to_all x4, starting transfers between devices, joined_exchange(): lax.all_to_all(blocks, axis, split_axis=0, concat_axis=0, tiled=True)  37.7 us
    all_to_all x2, blocking collectives, sent_and_summed(): lax.all_to_all(blocks, axis, split_axis=0, concat_axis=0, tiled=True)  20.5 us
    another operation x4, local copies, waits for them, and re-layouts, joined_exchange(): blocks = blocks.reshape(-1, *inside)  18.3 us
    dot_general x2, matrix products, expert_rows(): jnp.dot(hidden, down_weight, preferred_element_type=jnp.float32)  17.5 us
    convert_element_type x2, local copies, waits for them, and re-layouts, expert_rows(): partial_value.reshape(received.shape).astype(jnp.bfloat16)  13.8 us
    transpose x2, local copies, waits for them, and re-layouts, in_blocks(): return jnp.moveaxis(blocks, dim, 0)  9.18 us
    convert_element_type x2, other arithmetic, dequantize(): return product.reshape(blocks * 32, cols).astype(jnp.bfloat16)  8.9 us
  transfers between devices with their start and end apart: 4, of which 4 were waited for; matrix products, arithmetic and copies ran while one was open for 14% of the time, Pallas kernels for 0%

commit v1 on v0

v1 whole, which is shorter than its diff:
```python
import jax
import jax.numpy as jnp
from jax import lax
from jax.experimental import pallas as pl
from jax.experimental.pallas import tpu as pltpu
from jax.sharding import PartitionSpec as P

D = 2880
HALF = D // 2
HW2 = 768
E = 128
TOK = 64
TOP = 4
SUB = 8
LANES = 1152
THIRD = 384
WIDE = 1536
CHUNK = 256
BF = jnp.bfloat16
F32 = jnp.float32


def iota(shape, dim):
    return lax.broadcasted_iota(jnp.int32, shape, dim)


def one_hot(cond, dtype=BF):
    return jnp.where(cond, 1.0, 0.0).astype(dtype)


def dot(a, b, ca=1, cb=0):
    return lax.dot_general(a, b, (((ca,), (cb,)), ((), ())), preferred_element_type=F32)


def wanted(p, b, i):
    q = jnp.where(p < 6, p, 3 * (p - 6) + i)
    return jnp.where(b == (q & 1) + jnp.where(p < 6, 0, 2), (q >> 1) + 1, -1).astype(F32)


def placement(h, mig):
    named_from = one_hot(mig[0:1, :] == iota((E, mig.shape[1]), 0))
    named_to = one_hot(mig[1:2, :] == iota((E, mig.shape[1]), 0))
    moved = dot(named_from, named_to, 1, 1)
    named = dot(jnp.ones((SUB, mig.shape[1]), BF), named_to, 1, 1)[0:1, :]
    eye = one_hot(iota((E, E), 0) == iota((E, E), 1), F32)
    hf = h.astype(F32)
    return (moved * hf + eye * (1.0 - hf * named)).astype(BF)


def slot_codes(place, ids):
    owner = jnp.zeros((E, TOK), F32)
    for k in range(TOP):
        owner = owner + one_hot(ids[k : k + 1, :] == iota((E, TOK), 0), F32)
    named = dot(place, owner.astype(BF)).astype(BF)
    earlier = one_hot(iota((TOK, TOK), 0) < iota((TOK, TOK), 1))
    rank = dot(named, earlier)
    return (named.astype(F32) * (rank + 1.0)).astype(BF)


def third(ref, i):
    return ref.at[:, i * THIRD : (i + 1) * THIRD]


def pack_body(h_ref, ids_ref, mig_ref, tok_ref, out_ref, zero_ref, tok, tail, rows, sems):
    h = h_ref[0]
    load = pltpu.make_async_copy(tok_ref.at[h], tok, sems.at[3])
    load.start()
    zero_ref[...] = jnp.zeros(zero_ref.shape, BF)
    codes = slot_codes(placement(h, mig_ref[...]), ids_ref[h])
    repeat = one_hot((iota((TOK, 4 * TOK), 1) & (TOK - 1)) == iota((TOK, 4 * TOK), 0))
    spread = one_hot((iota((E * SUB, E), 0) >> 3) == iota((E * SUB, E), 1))
    codes = dot(spread, dot(codes, repeat).astype(BF)).reshape(E, SUB, 4 * TOK)
    p = iota((SUB, 4 * TOK), 0)
    b = iota((SUB, 4 * TOK), 1) >> 6
    load.wait()
    left = D - WIDE - LANES
    tail[:, 0:left] = tok[:, WIDE + LANES : D]
    tail[:, left:THIRD] = jnp.zeros((TOK, THIRD - left), BF)
    stores = []
    for i in range(3):
        select = one_hot(codes == wanted(p, b, i)[None]).reshape(E * SUB, 4 * TOK)
        source = jnp.concatenate(
            [
                tok[:, i * THIRD : (i + 1) * THIRD],
                tok[:, WIDE + i * THIRD : WIDE + (i + 1) * THIRD],
                tok[:, LANES:WIDE],
                tail[...],
            ],
            axis=0,
        )
        rows[:, i * THIRD : (i + 1) * THIRD] = dot(select, source).astype(BF)
        stores.append(pltpu.make_async_copy(third(rows, i), third(out_ref, i), sems.at[i]))
        stores[i].start()
    for store in stores:
        store.wait()


VMEM = pl.BlockSpec(memory_space=pltpu.VMEM)
SMEM = pl.BlockSpec(memory_space=pltpu.SMEM)
ANY = pl.BlockSpec(memory_space=pl.ANY)


def pack(h, ids, mig, tokens):
    return pl.pallas_call(
        pack_body,
        in_specs=[SMEM, VMEM, VMEM, ANY],
        out_specs=[ANY, VMEM],
        scratch_shapes=[
            pltpu.VMEM((TOK, D), BF),
            pltpu.VMEM((TOK, THIRD), BF),
            pltpu.VMEM((E * SUB, LANES), BF),
            pltpu.SemaphoreType.DMA((4,)),
        ],
        out_shape=[
            jax.ShapeDtypeStruct((E * SUB, LANES), BF),
            jax.ShapeDtypeStruct((16, 128), BF),
        ],
        name="pack",
        compiler_params=pltpu.CompilerParams(vmem_limit_bytes=24 << 20),
    )(h, ids, mig, tokens)


def mix_body(h_ref, ids_ref, mig_ref, gates_ref, out_ref):
    ids = ids_ref[h_ref[0]]
    gates = gates_ref[h_ref[0]]
    place = placement(h_ref[0], mig_ref[...])
    codes = slot_codes(place, ids)
    gate = jnp.zeros((E, TOK), F32)
    for k in range(TOP):
        gate = gate + jnp.where(ids[k : k + 1, :] == iota((E, TOK), 0), gates[k : k + 1, :], 0.0)
    high = gate.astype(BF)
    low = (gate - high.astype(F32)).astype(BF)
    repeat = one_hot((iota((4 * TOK, TOK), 0) & (TOK - 1)) == iota((4 * TOK, TOK), 1))
    spread = one_hot((iota((E, E * SUB), 1) >> 3) == iota((E, E * SUB), 0))

    def widened(x):
        return dot(dot(repeat, x, 1, 1).astype(BF), spread)

    codes = widened(codes)
    high = widened(dot(place, high).astype(BF))
    low = widened(dot(place, low).astype(BF))
    p = iota((4 * TOK, E * SUB), 1) & (SUB - 1)
    b = iota((4 * TOK, E * SUB), 0) >> 6
    for i in range(3):
        hit = codes == wanted(p, b, i)
        out_ref[i, 0 : 4 * TOK, :] = jnp.where(hit, high, 0.0).astype(BF)
        out_ref[i, 4 * TOK : 8 * TOK, :] = jnp.where(hit, low, 0.0).astype(BF)


def mix_weights(h, ids, mig, gates):
    return pl.pallas_call(
        mix_body,
        in_specs=[SMEM, VMEM, VMEM, VMEM],
        out_specs=VMEM,
        out_shape=jax.ShapeDtypeStruct((3, 8 * TOK, E * SUB), BF),
        name="mix_weights",
        compiler_params=pltpu.CompilerParams(vmem_limit_bytes=24 << 20),
    )(h, ids, mig, gates)


def pieces():
    for q in range(6):
        j, g = q // 2, q % 2
        for part in range(WIDE // 128):
            if part < 9:
                yield j, g * WIDE + part * 128, part, q
            else:
                yield j, g * WIDE + part * 128, 3 * (q % 3) + part - 9, 6 + q // 3


def expert_body(
    in_ref, up_a_hbm, up_b_hbm, down_a_hbm, down_b_hbm, out_hbm,
    wide, rows, hidden, out_ref, up_a, up_b, down_a, down_b, up_sems, down_sems, out_sems,
):
    ups, downs, stores = [], [], []
    for n, (src, dst) in enumerate(((up_a_hbm, up_a), (up_b_hbm, up_b))):
        for c in range(HW2 // CHUNK):
            cut = (slice(None), pl.ds(c * CHUNK, CHUNK))
            ups.append(pltpu.make_async_copy(src.at[cut], dst.at[cut], up_sems.at[len(ups)]))
    for n, (src, dst) in enumerate(((down_a_hbm, down_a), (down_b_hbm, down_b))):
        downs.append(pltpu.make_async_copy(src, dst, down_sems.at[n]))
    for load in ups + downs:
        load.start()
    for part in range(LANES // 128):
        wide[part] = in_ref[:, part * 128 : (part + 1) * 128].astype(F32)
    for j, lane, part, p in pieces():
        rows[j * E : (j + 1) * E, lane : lane + 128] = wide[part, pl.ds(p, E, stride=SUB), :].astype(BF)
    for n, up_ref in enumerate((up_a, up_b)):
        for c in range(HW2 // CHUNK):
            ups[n * (HW2 // CHUNK) + c].wait()
            pre = dot(rows[:, 0:D], up_ref[:, c * CHUNK : (c + 1) * CHUNK])
            act = pre / (1.0 + jnp.exp(-1.702 * pre))
            hidden[:, n * HW2 + c * CHUNK : n * HW2 + (c + 1) * CHUNK] = act.astype(BF)

    for load in downs:
        load.wait()

    def down(n0, n1):
        return dot(hidden[:, 0:HW2], down_a[n0:n1, :], 1, 1) + dot(hidden[:, HW2 : 2 * HW2], down_b[n0:n1, :], 1, 1)

    for g in range(2):
        y = down(g * HALF + LANES, (g + 1) * HALF)
        for j in range(3):
            q = 2 * j + g
            mine = y[j * E : (j + 1) * E]
            to = pl.ds(6 + q // 3, E, stride=SUB)
            wide[3 * (q % 3), to, :] = mine[:, 0:128]
            wide[3 * (q % 3) + 1, to, :] = mine[:, 128:256]
            last = jnp.concatenate([mine[:, 256:288], jnp.zeros((E, 96), F32)], axis=1)
            wide[3 * (q % 3) + 2, to, :] = last
    for i in range(3):
        for g in range(2):
            y = down(g * HALF + i * THIRD, g * HALF + (i + 1) * THIRD)
            for j in range(3):
                for part in range(3):
                    mine = y[j * E : (j + 1) * E, part * 128 : (part + 1) * 128]
                    wide[3 * i + part, pl.ds(2 * j + g, E, stride=SUB), :] = mine
        for part in range(3 * i, 3 * i + 3):
            out_ref[:, part * 128 : (part + 1) * 128] = wide[part].astype(BF)
        stores.append(pltpu.make_async_copy(third(out_ref, i), third(out_hbm, i), out_sems.at[i]))
        stores[i].start()
    for store in stores:
        store.wait()


def on_chip(x):
    return pltpu.with_memory_space_constraint(x, pltpu.VMEM)


def expert(received, up_a, up_b, down_a, down_b):
    return pl.pallas_call(
        expert_body,
        in_specs=[VMEM, ANY, ANY, ANY, ANY],
        out_specs=ANY,
        scratch_shapes=[
            pltpu.VMEM((LANES // 128, E * SUB, 128), F32),
            pltpu.VMEM((3 * E, 2 * WIDE), BF),
            pltpu.VMEM((3 * E, 2 * HW2), BF),
            pltpu.VMEM((E * SUB, LANES), BF),
        ]
        + [pltpu.VMEM((D, HW2), BF)] * 4
        + [pltpu.SemaphoreType.DMA((2 * HW2 // CHUNK,)), pltpu.SemaphoreType.DMA((2,)), pltpu.SemaphoreType.DMA((3,))],
        out_shape=jax.ShapeDtypeStruct((E * SUB, LANES), BF),
        name="expert",
        compiler_params=pltpu.CompilerParams(vmem_limit_bytes=44 << 20),
    )(on_chip(received), up_a, up_b, down_a, down_b)


def combine_body(h_ref, weights_ref, in_ref, full_ref, send_ref):
    h = h_ref[0]
    mains, tail = [], 0.0
    for i in range(3):
        out = dot(weights_ref[i], in_ref[:, i * THIRD : (i + 1) * THIRD])
        out = out[0 : 4 * TOK] + out[4 * TOK : 8 * TOK]
        mains.append(out[0 : 2 * TOK])
        tail = tail + out[2 * TOK : 4 * TOK]
    for g in range(2):
        own = slice(g * TOK, (g + 1) * TOK)

        def put(ref, own=own):
            for i in range(3):
                ref[:, i * THIRD : (i + 1) * THIRD] = mains[i][own].astype(BF)
            ref[:, LANES:HALF] = tail[own, 0 : HALF - LANES].astype(BF)

        @pl.when(h == g)
        def _():
            put(full_ref.at[g])

        @pl.when(h != g)
        def _():
            put(send_ref)


def combine(h, weights, returned):
    return pl.pallas_call(
        combine_body,
        in_specs=[SMEM, VMEM, VMEM],
        out_specs=[VMEM, VMEM],
        out_shape=[
            jax.ShapeDtypeStruct((2, TOK, HALF), BF),
            jax.ShapeDtypeStruct((TOK, HALF), BF),
        ],
        name="combine",
        compiler_params=pltpu.CompilerParams(vmem_limit_bytes=24 << 20),
    )(h, weights, on_chip(returned))


def finish_body(h_ref, full_ref, other_ref, out_ref, sem):
    copy = pltpu.make_async_copy(other_ref, out_ref.at[1 - h_ref[0]], sem)
    copy.start()
    copy.wait()


def finish(h, full, other):
    return pl.pallas_call(
        finish_body,
        in_specs=[SMEM, ANY, VMEM],
        out_specs=ANY,
        scratch_shapes=[pltpu.SemaphoreType.DMA(())],
        out_shape=jax.ShapeDtypeStruct(full.shape, BF),
        input_output_aliases={1: 0},
        name="finish",
    )(h, full, on_chip(other))


def exchange(x):
    blocks = x.reshape(E, SUB, LANES)
    return lax.all_to_all(blocks, ("col", "row"), 0, 0, tiled=True).reshape(E * SUB, LANES)


def swapped(x):
    return lax.ppermute(x, "pair", [(0, 1), (1, 0)])


def dequantize_up(values, scales):
    shaped = values.reshape(D // 32, 32, HW2).astype(F32) * scales.astype(F32)[:, None, :]
    return shaped.astype(BF).reshape(D, HW2)


def dequantize_down(values, scales):
    group = (iota((HW2 // 32, HW2), 1) // 32 == iota((HW2 // 32, HW2), 0)).astype(BF)
    spread = jnp.einsum("bn,bk->nk", scales, group, preferred_element_type=F32)
    return (values.T.astype(F32) * spread).astype(BF)


def per_device(
    tokens, expert_ids, gate_weights, migration, up_values, up_scales, down_values, down_scales
):
    own = lax.axis_index("pair")
    h = own.astype(jnp.int32).reshape(1)
    ids = expert_ids.transpose(0, 2, 1)
    gates = gate_weights.transpose(0, 2, 1)
    mig = migration.T
    packed, zero = pack(h, ids, mig, tokens)
    received = exchange(packed)
    up_a = dequantize_up(up_values[0], up_scales[0] + zero[0, 0])
    down_a = dequantize_down(down_values[0], down_scales[0] + zero[0, 0])
    up_b = swapped(up_a)
    down_b = swapped(down_a)
    weights = mix_weights(h, ids, mig, gates)
    returned = exchange(expert(received, up_a, up_b, down_a, down_b))
    full, send = combine(h, weights, returned)
    return finish(h, full, swapped(send))


def solution(mesh):
    placed = (
        P(None, ("col", "row"), None),
        P(None, ("col", "row"), None),
        P(None, ("col", "row"), None),
        P(),
        P(("col", "row"), None, "pair"),
        P(("col", "row"), None, "pair"),
        P(("col", "row"), "pair", None),
        P(("col", "row"), "pair", None),
    )
    return jax.shard_map(
        per_device,
        mesh=mesh,
        in_specs=placed,
        out_specs=P(None, ("col", "row"), "pair"),
        check_vma=False,
    )
```

time: 367 us -> 176 us (0.48); the launches traced: 361 us -> 175 us
  waiting for transfers between devices: 176 us -> 98.1 us
  local copies, waits for them, and re-layouts: 83 us -> 12.2 us
  Pallas kernels: 0 us -> 25.7 us
  blocking collectives: 20.5 us -> 0 us
  matrix products: 22.5 us -> 4.3 us
  other arithmetic: 20.5 us -> 3.81 us
  starting transfers between devices: 37.7 us -> 30.6 us
    all_to_all x4 -> x2, waiting for transfers between devices: 176 us -> 92.4 us  [exchange(): lax.all_to_all(blocks, ('col', 'row'), 0, 0, tiled=True)]
    another operation x14 -> x0, local copies, waits for them, and re-layouts: 30.1 us -> none  [the longest x4 18.3 us: joined_exchange(): blocks = blocks.reshape(-1, *inside)]
    pallas_call x0 -> x5, Pallas kernels: none -> 25.7 us  [the longest x1 16.1 us: expert(): pl.pallas_call(expert_body, in_specs=[VMEM, ANY, ANY, ANY, ANY], out_spec...]
    all_to_all x2 -> x0, blocking collectives: 20.5 us -> none  [sent_and_summed(): lax.all_to_all(blocks, axis, split_axis=0, concat_axis=0, tiled=True)]
    convert_element_type x4 -> x0, local copies, waits for them, and re-layouts: 20.5 us -> none  [the longest x2 13.8 us: expert_rows(): partial_value.reshape(received.shape).astype(jnp.bfloat16)]
    dot_general x4 -> x1, matrix products: 22.5 us -> 4.3 us  [dequantize_down(): spread = jnp.einsum('bn,bk->nk', scales, group, preferred_element_type=F32)]
    all_to_all x4 -> x2, starting transfers between devices: 37.7 us -> 24 us  [exchange(): lax.all_to_all(blocks, ('col', 'row'), 0, 0, tiled=True)]
    transpose x2 -> x0, local copies, waits for them, and re-layouts: 9.18 us -> none  [in_blocks(): return jnp.moveaxis(blocks, dim, 0)]
  transfers between devices with their start and end apart: 4 -> 5, of which waited for: 4 -> 5; matrix products, arithmetic and copies ran while one was open for 14% -> 5% of each run, Pallas kernels for 0% -> 1%
where the time goes in v1:
time: 176 us; the launch traced here: 175 us
  waiting for transfers between devices  98.1 us (56%)
  starting transfers between devices  30.6 us (17%)
  Pallas kernels  25.7 us (15%)
  local copies, waits for them, and re-layouts  12.2 us (7%)
  matrix products  4.3 us (2%)
  other arithmetic  3.81 us (2%)
    all_to_all x2, waiting for transfers between devices, exchange(): lax.all_to_all(blocks, ('col', 'row'), 0, 0, tiled=True)  92.4 us
    all_to_all x2, starting transfers between devices, exchange(): lax.all_to_all(blocks, ('col', 'row'), 0, 0, tiled=True)  24 us
    pallas_call x1, Pallas kernels, expert(): pl.pallas_call(expert_body, in_specs=[VMEM, ANY, ANY, ANY, ANY], out_spec...  16.1 us
    unnamed x28, local copies, waits for them, and re-layouts  11.7 us
    ppermute x3, starting transfers between devices, swapped(): return lax.ppermute(x, 'pair', [(0, 1), (1, 0)])  6.62 us
    ppermute x3, waiting for transfers between devices, swapped(): return lax.ppermute(x, 'pair', [(0, 1), (1, 0)])  5.65 us
    dot_general x1, matrix products, dequantize_down(): spread = jnp.einsum('bn,bk->nk', scales, group, preferred_element_type=F32)  4.3 us
    pallas_call x1, Pallas kernels, combine(): pl.pallas_call(combine_body, in_specs=[SMEM, VMEM, VMEM], out_specs=[VMEM...  4.24 us
  transfers between devices with their start and end apart: 5, of which 5 were waited for; matrix products, arithmetic and copies ran while one was open for 5% of the time, Pallas kernels for 1%

profile of v1, /device:TPU:1, one launch (start us, length us, event | category | flops | bytes accessed | tf_op | source)
XLA Modules:
  0.0 175.1 jit_solution(11089378930149439377)
XLA Ops:
  0.0 1.1 copy-done.4
  1.1 0.7 copy-done.5
  2.5 2.6 %pack.1 = (bf16[1024,1152]{1,0:T(8,128)(2,1)S(1)}, bf16[16,128]{1,0:T(8,128)(2,1)S(1)}) custom-call(s32[1]{0:T(128)} %bitcast.h_ref, s32[2,4,64]{2,1,0:T(4,128)S(1)} %bitcast.32, s32[2,32]{1,0:T(2,128)S(1)} %bitcast.34, bf16[2,64,2880]{2,1,0:T(8,128)(2,1)S(1)} %copy-done.4), custom_call_target="tpu_custom_call" | custom-call | tf_op jit(solution)/shard_map/pack/pallas_call | solution.py:104
  5.1 1.4 copy-done.3
  6.5 16.3 %all-to-all-start = ((bf16[128,8,1152]{2,1,0:T(8,128)(2,1)}), bf16[128,8,1152]{2,1,0:T(8,128)(2,1)S(1)}, u32[]{:S(2)}, u32[]{:S(2)}) async-start(bf16[128,8,1152]{2,1,0:T(8,128)(2,1)} %bitcast.31), calls=%async_computation | async-start | bytes 4718592 | tf_op jit(solution)/shard_map/all_to_all | solution.py:308
  23.3 4.3 %fusion.1.down_a_hbm = bf16[2880,768]{1,0:T(8,128)(2,1)S(1)} fusion(bf16[1,768,2880]{1,2,0:T(8,128)(2,1)} %param.14, bf16[1,24,2880]{2,1,0:T(8,128)(2,1)S(1)} %copy-done.13, bf16[]{:T(256)} %bitcast.7, s32[768]{0:T(1024)S(1)} %get-tuple-element.13, s32[768]{0:T(1024)S(1)} %get-tuple-element.14, pred[768]{0:T(1024)(128)(4,1)S(1)} %fusion.11), kind=kOutput, calls=%fused_computation.2 | convolution fusion | flops 112909824 | bytes 8992514 | tf_op jit(solution)/shard_map/bn,bk->nk/dot_general | solution.py:322
  27.7 1.0 collective-permute-start.1
  28.7 0.7 bitcast_convert_fusion
  29.4 3.1 %fusion.2.up_a_hbm = bf16[2880,768]{1,0:T(8,128)(2,1)S(1)} fusion(bf16[1,2880,768]{2,1,0:T(8,128)(2,1)} %param.12, f32[90,768]{1,0:T(8,128)S(1)} %bitcast_convert_fusion), kind=kLoop, calls=%fused_computation.4 | loop fusion | flops 6635520 | bytes 9123840 | tf_op jit(solution)/shard_map/convert_element_type | solution.py:317
  32.5 1.0 collective-permute-start
  33.5 2.0 %copy-done = bf16[2880,768]{1,0:T(8,128)(2,1)} copy-done((bf16[2880,768]{1,0:T(8,128)(2,1)}, bf16[2880,768]{1,0:T(8,128)(2,1)S(1)}, u32[]{:S(2)}) %copy-start) | copy-done | bytes 4423704
  35.8 2.1 %copy-done.11 = bf16[2880,768]{1,0:T(8,128)(2,1)} copy-done((bf16[2880,768]{1,0:T(8,128)(2,1)}, bf16[2880,768]{1,0:T(8,128)(2,1)S(1)}, u32[]{:S(2)}) %copy-start.11) | copy-done | bytes 4423704
  37.9 4.3 %collective-permute-done.up_b_hbm = bf16[2880,768]{1,0:T(8,128)(2,1)} collective-permute-done((bf16[2880,768]{1,0:T(8,128)(2,1)S(1)}, bf16[2880,768]{1,0:T(8,128)(2,1)}, u32[]{:S(2)}, u32[]{:S(2)}) %collective-permute-start) | collective-permute-done | bytes 4423712 | tf_op jit(solution)/shard_map/ppermute | solution.py:312
  42.3 38.8 %all-to-all-done = bf16[128,8,1152]{2,1,0:T(8,128)(2,1)S(1)} async-done(((bf16[128,8,1152]{2,1,0:T(8,128)(2,1)}), bf16[128,8,1152]{2,1,0:T(8,128)(2,1)S(1)}, u32[]{:S(2)}, u32[]{:S(2)}) %all-to-all-start) | async-done | bytes 2359328 | tf_op jit(solution)/shard_map/all_to_all | solution.py:308
  81.1 2.3 %copy-done.1 = bf16[2880,768]{1,0:T(8,128)(2,1)S(1)} copy-done((bf16[2880,768]{1,0:T(8,128)(2,1)S(1)}, bf16[2880,768]{1,0:T(8,128)(2,1)}, u32[]{:S(2)}) %copy-start.1) | copy-done | bytes 4423704
  83.4 16.1 %expert.1 = bf16[1024,1152]{1,0:T(8,128)(2,1)S(1)} custom-call(bf16[1024,1152]{1,0:T(8,128)(2,1)S(1)} %bitcast.29, bf16[2880,768]{1,0:T(8,128)(2,1)S(1)} %copy-done.1, bf16[2880,768]{1,0:T(8,128)(2,1)} %collective-permute-done.up_b_hbm, bf16[2880,768]{1,0:T(8,128)(2,1)} %copy-done.10, bf16[2880,768]{1,0:T(8,128)(2,1)} %copy-done.11), custom_call_target="tpu_custom_call" | custom-call | tf_op jit(solution)/shard_map/expert/pallas_call | solution.py:231
  99.4 1.4 copy-done.2
  100.9 7.6 %all-to-all-start.1 = ((bf16[128,8,1152]{2,1,0:T(8,128)(2,1)}), bf16[128,8,1152]{2,1,0:T(8,128)(2,1)}, u32[]{:S(2)}, u32[]{:S(2)}) async-start(bf16[128,8,1152]{2,1,0:T(8,128)(2,1)} %bitcast.30), calls=%async_computation.1 | async-start | bytes 4718592 | tf_op jit(solution)/shard_map/all_to_all | solution.py:308
  108.6 2.2 %mix_weights.1.weights_ref = bf16[3,512,1024]{2,1,0:T(8,128)(2,1)S(1)} custom-call(s32[1]{0:T(128)} %bitcast.h_ref, s32[2,4,64]{2,1,0:T(4,128)S(1)} %bitcast.33, s32[2,32]{1,0:T(2,128)S(1)} %bitcast.35, f32[2,4,64]{2,1,0:T(4,128)S(1)} %bitcast.36), custom_call_target="tpu_custom_call" | custom-call | tf_op jit(solution)/shard_map/mix_weights/pallas_call | solution.py:151
  110.7 53.6 %all-to-all-done.1 = bf16[128,8,1152]{2,1,0:T(8,128)(2,1)} async-done(((bf16[128,8,1152]{2,1,0:T(8,128)(2,1)}), bf16[128,8,1152]{2,1,0:T(8,128)(2,1)}, u32[]{:S(2)}, u32[]{:S(2)}) %all-to-all-start.1) | async-done | bytes 2359328 | tf_op jit(solution)/shard_map/all_to_all | solution.py:308
  164.3 4.2 %combine.1 = (bf16[2,64,1440]{2,1,0:T(8,128)(2,1)}, bf16[64,1440]{1,0:T(8,128)(2,1)S(1)}) custom-call(s32[1]{0:T(128)} %bitcast.h_ref, bf16[3,512,1024]{2,1,0:T(8,128)(2,1)S(1)} %mix_weights.1.weights_ref, bf16[1024,1152]{1,0:T(8,128)(2,1)} %bitcast.14.in_ref), custom_call_target="tpu_custom_call" | custom-call | tf_op jit(solution)/shard_map/combine/pallas_call | solution.py:275
  168.6 4.6 %collective-permute-start.2 = (bf16[64,1440]{1,0:T(8,128)(2,1)S(1)}, bf16[64,1440]{1,0:T(8,128)(2,1)S(1)}, u32[]{:S(2)}, u32[]{:S(2)}) collective-permute-start(bf16[64,1440]{1,0:T(8,128)(2,1)S(1)} %get-tuple-element.12), channel_id=1, source_target_pairs={{0,1},{1,0},{2,3},{3,2},{4,5},{5,4},{6,7},{7,6},{8,9},{9,8},{10,11... | collective-permute-start | bytes 552968 | tf_op jit(solution)/shard_map/ppermute | solution.py:312
  173.1 1.1 collective-permute-done.2.other_ref
  174.2 0.7 finish.1
  (25 shorter events, 1.5 us)
Async XLA Ops:
  0.0 1.1 copy-start.4
  1.1 0.7 copy-start.5
  1.8 0.7 copy-start.7
  2.5 20.8 %copy-start.13 = (bf16[1,24,2880]{2,1,0:T(8,128)(2,1)S(1)}, bf16[1,24,2880]{2,1,0:T(8,128)(2,1)}, u32[]{:S(2)}) copy-start(bf16[1,24,2880]{2,1,0:T(8,128)(2,1)} %param.15) | copy-start | bytes 414724
  5.1 1.4 copy-start.3
  6.5 74.7 %all-to-all-start = ((bf16[128,8,1152]{2,1,0:T(8,128)(2,1)}), bf16[128,8,1152]{2,1,0:T(8,128)(2,1)S(1)}, u32[]{:S(2)}, u32[]{:S(2)}) async-start(bf16[128,8,1152]{2,1,0:T(8,128)(2,1)} %bitcast.31), calls=%async_computation | async-start | bytes 4718592 | tf_op jit(solution)/shard_map/all_to_all | solution.py:308
  23.3 5.4 %copy-start.12 = (bf16[1,90,768]{2,1,0:T(8,128)(2,1)S(1)}, bf16[1,90,768]{2,1,0:T(8,128)(2,1)}, u32[]{:S(2)}) copy-start(bf16[1,90,768]{2,1,0:T(8,128)(2,1)} %param.13) | copy-start | bytes 414724
  27.6 4.9 %copy-start.10 = (bf16[2880,768]{1,0:T(8,128)(2,1)}, bf16[2880,768]{1,0:T(8,128)(2,1)S(1)}, u32[]{:S(2)}) copy-start(bf16[2880,768]{1,0:T(8,128)(2,1)S(1)} %fusion.1.down_a_hbm) | copy-start | bytes 13271044
  27.7 8.1 %collective-permute-start.1 = (bf16[2880,768]{1,0:T(8,128)(2,1)S(1)}, bf16[2880,768]{1,0:T(8,128)(2,1)S(1)}, u32[]{:S(2)}, u32[]{:S(2)}) collective-permute-start(bf16[2880,768]{1,0:T(8,128)(2,1)S(1)} %fusion.1.down_a_hbm), channel_id=1, source_target_pairs={{0,1},{1,0},{2,3},{3,2},{4,5},{5,4},{6,7},{7,6},{8,9},{9,8},{10,11... | collective-permute-start | bytes 13271048 | tf_op jit(solution)/shard_map/ppermute | solution.py:312
  32.5 9.8 %collective-permute-start = (bf16[2880,768]{1,0:T(8,128)(2,1)S(1)}, bf16[2880,768]{1,0:T(8,128)(2,1)}, u32[]{:S(2)}, u32[]{:S(2)}) collective-permute-start(bf16[2880,768]{1,0:T(8,128)(2,1)S(1)} %fusion.2.up_a_hbm), channel_id=1, source_target_pairs={{0,1},{1,0},{2,3},{3,2},{4,5},{5,4},{6,7},{7,6},{8,9},{9,8},{10,11... | collective-permute-start | bytes 13271048 | tf_op jit(solution)/shard_map/ppermute | solution.py:312
  33.5 2.0 %copy-start = (bf16[2880,768]{1,0:T(8,128)(2,1)}, bf16[2880,768]{1,0:T(8,128)(2,1)S(1)}, u32[]{:S(2)}) copy-start(bf16[2880,768]{1,0:T(8,128)(2,1)S(1)} %fusion.2.up_a_hbm) | copy-start | bytes 13271044
  35.8 2.1 %copy-start.11 = (bf16[2880,768]{1,0:T(8,128)(2,1)}, bf16[2880,768]{1,0:T(8,128)(2,1)S(1)}, u32[]{:S(2)}) copy-start(bf16[2880,768]{1,0:T(8,128)(2,1)S(1)} %collective-permute-done.1.down_b_hbm) | copy-start | bytes 13271044
  81.1 2.3 %copy-start.1 = (bf16[2880,768]{1,0:T(8,128)(2,1)S(1)}, bf16[2880,768]{1,0:T(8,128)(2,1)}, u32[]{:S(2)}) copy-start(bf16[2880,768]{1,0:T(8,128)(2,1)} %copy-done) | copy-start | bytes 13271044
  99.4 1.4 copy-start.2
  100.9 7.7 %copy-start.6 = (s32[2,64,4]{1,2,0:T(4,128)S(1)}, s32[2,64,4]{1,2,0:T(4,128)}, u32[]{:S(2)}) copy-start(s32[2,64,4]{1,2,0:T(4,128)} %param.9) | copy-start | bytes 6148
  100.9 7.7 %copy-start.8 = (s32[32,2]{0,1:T(2,128)S(1)}, s32[32,2]{0,1:T(2,128)}, u32[]{:S(2)}) copy-start(s32[32,2]{0,1:T(2,128)} %param.11) | copy-start | bytes 772
  100.9 7.7 %copy-start.9 = (f32[2,64,4]{1,2,0:T(4,128)S(1)}, f32[2,64,4]{1,2,0:T(4,128)}, u32[]{:S(2)}) copy-start(f32[2,64,4]{1,2,0:T(4,128)} %param.10) | copy-start | bytes 6148
  100.9 63.5 %all-to-all-start.1 = ((bf16[128,8,1152]{2,1,0:T(8,128)(2,1)}), bf16[128,8,1152]{2,1,0:T(8,128)(2,1)}, u32[]{:S(2)}, u32[]{:S(2)}) async-start(bf16[128,8,1152]{2,1,0:T(8,128)(2,1)} %bitcast.30), calls=%async_computation.1 | async-start | bytes 4718592 | tf_op jit(solution)/shard_map/all_to_all | solution.py:308
  168.6 5.6 %collective-permute-start.2 = (bf16[64,1440]{1,0:T(8,128)(2,1)S(1)}, bf16[64,1440]{1,0:T(8,128)(2,1)S(1)}, u32[]{:S(2)}, u32[]{:S(2)}) collective-permute-start(bf16[64,1440]{1,0:T(8,128)(2,1)S(1)} %get-tuple-element.12), channel_id=1, source_target_pairs={{0,1},{1,0},{2,3},{3,2},{4,5},{5,4},{6,7},{7,6},{8,9},{9,8},{10,11... | collective-permute-start | bytes 552968 | tf_op jit(solution)/shard_map/ppermute | solution.py:312

commit v2 on v1

--- a/solution.py
+++ b/solution.py
@@ -61,12 +61,20 @@
     return ref.at[:, i * THIRD : (i + 1) * THIRD]
 
 
-def pack_body(h_ref, ids_ref, mig_ref, tok_ref, out_ref, zero_ref, tok, tail, rows, sems):
+def pack_body(h_ref, ids_ref, mig_ref, tok_ref, out_ref, zero_ref, tok, tail, rows, ids, mig, sems):
     h = h_ref[0]
+    small = [
+        pltpu.make_async_copy(ids_ref.at[h], ids, sems.at[4]),
+        pltpu.make_async_copy(mig_ref, mig, sems.at[5]),
+    ]
+    for copy in small:
+        copy.start()
     load = pltpu.make_async_copy(tok_ref.at[h], tok, sems.at[3])
     load.start()
     zero_ref[...] = jnp.zeros(zero_ref.shape, BF)
-    codes = slot_codes(placement(h, mig_ref[...]), ids_ref[h])
+    for copy in small:
+        copy.wait()
+    codes = slot_codes(placement(h, mig[...]), ids[...])
     repeat = one_hot((iota((TOK, 4 * TOK), 1) & (TOK - 1)) == iota((TOK, 4 * TOK), 0))
     spread = one_hot((iota((E * SUB, E), 0) >> 3) == iota((E * SUB, E), 1))
     codes = dot(spread, dot(codes, repeat).astype(BF)).reshape(E, SUB, 4 * TOK)
@@ -97,27 +105,29 @@
 
 VMEM = pl.BlockSpec(memory_space=pltpu.VMEM)
 SMEM = pl.BlockSpec(memory_space=pltpu.SMEM)
-ANY = pl.BlockSpec(memory_space=pl.ANY)
+HBM = pl.BlockSpec(memory_space=pltpu.HBM)
 
 
 def pack(h, ids, mig, tokens):
     return pl.pallas_call(
         pack_body,
-        in_specs=[SMEM, VMEM, VMEM, ANY],
-        out_specs=[ANY, VMEM],
+        in_specs=[SMEM, HBM, HBM, HBM],
+        out_specs=[HBM, VMEM],
         scratch_shapes=[
             pltpu.VMEM((TOK, D), BF),
             pltpu.VMEM((TOK, THIRD), BF),
             pltpu.VMEM((E * SUB, LANES), BF),
-            pltpu.SemaphoreType.DMA((4,)),
+            pltpu.VMEM((TOP, TOK), jnp.int32),
+            pltpu.VMEM(mig.shape, jnp.int32),
+            pltpu.SemaphoreType.DMA((6,)),
         ],
         out_shape=[
-            jax.ShapeDtypeStruct((E * SUB, LANES), BF),
+            pltpu.HBM((E * SUB, LANES), BF),
             jax.ShapeDtypeStruct((16, 128), BF),
         ],
         name="pack",
         compiler_params=pltpu.CompilerParams(vmem_limit_bytes=24 << 20),
-    )(h, ids, mig, tokens)
+    )(h, in_hbm(ids), in_hbm(mig), in_hbm(tokens))
 
 
 def mix_body(h_ref, ids_ref, mig_ref, gates_ref, out_ref):
@@ -198,31 +208,42 @@
     def down(n0, n1):
         return dot(hidden[:, 0:HW2], down_a[n0:n1, :], 1, 1) + dot(hidden[:, HW2 : 2 * HW2], down_b[n0:n1, :], 1, 1)
 
+    def put(y, g, i0, i1):
+        for j in range(3):
+            for part in range(3 * i0, 3 * i1):
+                lane = (part - 3 * i0) * 128
+                wide[part, pl.ds(2 * j + g, E, stride=SUB), :] = y[j * E : (j + 1) * E, lane : lane + 128]
+
+    def send(i):
+        for part in range(3 * i, 3 * i + 3):
+            out_ref[:, part * 128 : (part + 1) * 128] = wide[part].astype(BF)
+        stores.append(pltpu.make_async_copy(third(out_ref, i), third(out_hbm, i), out_sems.at[i]))
+        stores[-1].start()
+
     for g in range(2):
-        y = down(g * HALF + LANES, (g + 1) * HALF)
+        y = down(g * HALF + 2 * THIRD, (g + 1) * HALF)
+        put(y, g, 2, 3)
         for j in range(3):
             q = 2 * j + g
-            mine = y[j * E : (j + 1) * E]
+            mine = y[j * E : (j + 1) * E, THIRD:]
             to = pl.ds(6 + q // 3, E, stride=SUB)
             wide[3 * (q % 3), to, :] = mine[:, 0:128]
             wide[3 * (q % 3) + 1, to, :] = mine[:, 128:256]
             last = jnp.concatenate([mine[:, 256:288], jnp.zeros((E, 96), F32)], axis=1)
             wide[3 * (q % 3) + 2, to, :] = last
-    for i in range(3):
-        for g in range(2):
-            y = down(g * HALF + i * THIRD, g * HALF + (i + 1) * THIRD)
-            for j in range(3):
-                for part in range(3):
-                    mine = y[j * E : (j + 1) * E, part * 128 : (part + 1) * 128]
-                    wide[3 * i + part, pl.ds(2 * j + g, E, stride=SUB), :] = mine
-        for part in range(3 * i, 3 * i + 3):
-            out_ref[:, part * 128 : (part + 1) * 128] = wide[part].astype(BF)
-        stores.append(pltpu.make_async_copy(third(out_ref, i), third(out_hbm, i), out_sems.at[i]))
-        stores[i].start()
+    send(2)
+    for g in range(2):
+        put(down(g * HALF, g * HALF + 2 * THIRD), g, 0, 2)
+    send(0)
+    send(1)
     for store in stores:
         store.wait()
 
 
+def in_hbm(x):
+    return pltpu.with_memory_space_constraint(x, pltpu.HBM)
+
+
 def on_chip(x):
     return pltpu.with_memory_space_constraint(x, pltpu.VMEM)
 
@@ -230,8 +251,8 @@
 def expert(received, up_a, up_b, down_a, down_b):
     return pl.pallas_call(
         expert_body,
-        in_specs=[VMEM, ANY, ANY, ANY, ANY],
-        out_specs=ANY,
+        in_specs=[VMEM, HBM, HBM, HBM, HBM],
+        out_specs=HBM,
         scratch_shapes=[
             pltpu.VMEM((LANES // 128, E * SUB, 128), F32),
             pltpu.VMEM((3 * E, 2 * WIDE), BF),
@@ -240,10 +261,10 @@
         ]
         + [pltpu.VMEM((D, HW2), BF)] * 4
         + [pltpu.SemaphoreType.DMA((2 * HW2 // CHUNK,)), pltpu.SemaphoreType.DMA((2,)), pltpu.SemaphoreType.DMA((3,))],
-        out_shape=jax.ShapeDtypeStruct((E * SUB, LANES), BF),
+        out_shape=pltpu.HBM((E * SUB, LANES), BF),
         name="expert",
         compiler_params=pltpu.CompilerParams(vmem_limit_bytes=44 << 20),
-    )(on_chip(received), up_a, up_b, down_a, down_b)
+    )(on_chip(received), *[in_hbm(x) for x in (up_a, up_b, down_a, down_b)])
 
 
 def combine_body(h_ref, weights_ref, in_ref, full_ref, send_ref):
@@ -294,8 +315,8 @@
 def finish(h, full, other):
     return pl.pallas_call(
         finish_body,
-        in_specs=[SMEM, ANY, VMEM],
-        out_specs=ANY,
+        in_specs=[SMEM, HBM, VMEM],
+        out_specs=HBM,
         scratch_shapes=[pltpu.SemaphoreType.DMA(())],
         out_shape=jax.ShapeDtypeStruct(full.shape, BF),
         input_output_aliases={1: 0},

time: 176 us -> 168 us (0.955)
  local copies, waits for them, and re-layouts: 12.2 us -> 2.55 us
  waiting for transfers between devices: 98.1 us -> 100 us
    unnamed x28 -> x16, local copies, waits for them, and re-layouts: 11.7 us -> 2.04 us
    ppermute x3, waiting for transfers between devices: 5.65 us -> 7.79 us  [swapped(): return lax.ppermute(x, 'pair', [(0, 1), (1, 0)])]
where the time goes in v2:
time: 168 us
  waiting for transfers between devices  100 us (60%)
  starting transfers between devices  30.6 us (18%)
  Pallas kernels  26 us (15%)
  matrix products  4.3 us (3%)
  other arithmetic  3.82 us (2%)
  local copies, waits for them, and re-layouts  2.55 us (2%)
    all_to_all x2, waiting for transfers between devices, exchange(): lax.all_to_all(blocks, ('col', 'row'), 0, 0, tiled=True)  92.4 us
    all_to_all x2, starting transfers between devices, exchange(): lax.all_to_all(blocks, ('col', 'row'), 0, 0, tiled=True)  24 us
    pallas_call x1, Pallas kernels, expert(): pl.pallas_call(expert_body, in_specs=[VMEM, HBM, HBM, HBM, HBM], out_spec...  15.3 us
    ppermute x3, waiting for transfers between devices, swapped(): return lax.ppermute(x, 'pair', [(0, 1), (1, 0)])  7.79 us
    ppermute x3, starting transfers between devices, swapped(): return lax.ppermute(x, 'pair', [(0, 1), (1, 0)])  6.64 us
    dot_general x1, matrix products, dequantize_down(): spread = jnp.einsum('bn,bk->nk', scales, group, preferred_element_type=F32)  4.3 us
    pallas_call x1, Pallas kernels, combine(): pl.pallas_call(combine_body, in_specs=[SMEM, VMEM, VMEM], out_specs=[VMEM...  4.24 us
    pallas_call x1, Pallas kernels, pack(): pl.pallas_call(pack_body, in_specs=[SMEM, HBM, HBM, HBM], out_specs=[HBM,...  3.57 us
  transfers between devices with their start and end apart: 5, of which 5 were waited for; matrix products, arithmetic and copies ran while one was open for 5% of the time, Pallas kernels for 1%

profile of v2, /device:TPU:1, one launch (start us, length us, event | category | flops | bytes accessed | tf_op | source)
XLA Modules:
  0.0 167.8 jit_solution(982705376252375366)
XLA Ops:
  0.0 3.6 %pack.1 = (bf16[1024,1152]{1,0:T(8,128)(2,1)}, bf16[16,128]{1,0:T(8,128)(2,1)S(1)}) custom-call(s32[1]{0:T(128)} %bitcast.h_ref, s32[2,4,64]{2,1,0:T(4,128)} %bitcast.30, s32[2,32]{1,0:T(2,128)} %bitcast.32, bf16[2,64,2880]{2,1,0:T(8,128)(2,1)} %tok_ref.1), custom_call_target="tpu_custom_call" | custom-call | tf_op jit(solution)/shard_map/pack/pallas_call | solution.py:112
  3.6 16.3 %all-to-all-start = ((bf16[128,8,1152]{2,1,0:T(8,128)(2,1)}), bf16[128,8,1152]{2,1,0:T(8,128)(2,1)S(1)}, u32[]{:S(2)}, u32[]{:S(2)}) async-start(bf16[128,8,1152]{2,1,0:T(8,128)(2,1)} %bitcast.36), calls=%async_computation | async-start | bytes 4718592 | tf_op jit(solution)/shard_map/all_to_all | solution.py:329
  19.9 0.5 slice.4
  20.5 4.3 %fusion.1.down_a_hbm = bf16[2880,768]{1,0:T(8,128)(2,1)S(1)} fusion(bf16[1,768,2880]{1,2,0:T(8,128)(2,1)} %param.14, bf16[1,24,2880]{2,1,0:T(8,128)(2,1)S(1)} %copy-done.7, bf16[]{:T(256)} %bitcast.7, s32[768]{0:T(1024)S(1)} %get-tuple-element.13, s32[768]{0:T(1024)S(1)} %get-tuple-element.14, pred[768]{0:T(1024)(128)(4,1)S(1)} %fusion.11), kind=kOutput, calls=%fused_computation.2 | convolution fusion | flops 112909824 | bytes 8992514 | tf_op jit(solution)/shard_map/bn,bk->nk/dot_general | solution.py:343
  24.8 0.0 copy-start.4
  24.8 1.0 collective-permute-start.1
  25.8 0.7 bitcast_convert_fusion
  26.5 3.1 %fusion.2.up_a_hbm = bf16[2880,768]{1,0:T(8,128)(2,1)S(1)} fusion(bf16[1,2880,768]{2,1,0:T(8,128)(2,1)} %param.12, f32[90,768]{1,0:T(8,128)S(1)} %bitcast_convert_fusion), kind=kLoop, calls=%fused_computation.4 | loop fusion | flops 6635520 | bytes 9123840 | tf_op jit(solution)/shard_map/convert_element_type | solution.py:338
  29.7 1.0 collective-permute-start
  30.7 2.3 %collective-permute-done.1.down_b_hbm = bf16[2880,768]{1,0:T(8,128)(2,1)S(1)} collective-permute-done((bf16[2880,768]{1,0:T(8,128)(2,1)S(1)}, bf16[2880,768]{1,0:T(8,128)(2,1)S(1)}, u32[]{:S(2)}, u32[]{:S(2)}) %collective-permute-start.1) | collective-permute-done | bytes 4423712 | tf_op jit(solution)/shard_map/ppermute | solution.py:333
  32.9 2.0 %copy-done.5 = bf16[2880,768]{1,0:T(8,128)(2,1)} copy-done((bf16[2880,768]{1,0:T(8,128)(2,1)}, bf16[2880,768]{1,0:T(8,128)(2,1)S(1)}, u32[]{:S(2)}) %copy-start.5) | copy-done | bytes 4423704
  34.9 4.4 %collective-permute-done.up_b_hbm = bf16[2880,768]{1,0:T(8,128)(2,1)} collective-permute-done((bf16[2880,768]{1,0:T(8,128)(2,1)S(1)}, bf16[2880,768]{1,0:T(8,128)(2,1)}, u32[]{:S(2)}, u32[]{:S(2)}) %collective-permute-start) | collective-permute-done | bytes 4423712 | tf_op jit(solution)/shard_map/ppermute | solution.py:333
  39.4 38.8 %all-to-all-done = bf16[128,8,1152]{2,1,0:T(8,128)(2,1)S(1)} async-done(((bf16[128,8,1152]{2,1,0:T(8,128)(2,1)}), bf16[128,8,1152]{2,1,0:T(8,128)(2,1)S(1)}, u32[]{:S(2)}, u32[]{:S(2)}) %all-to-all-start) | async-done | bytes 2359328 | tf_op jit(solution)/shard_map/all_to_all | solution.py:329
  78.2 15.3 %expert.1 = bf16[1024,1152]{1,0:T(8,128)(2,1)} custom-call(bf16[1024,1152]{1,0:T(8,128)(2,1)S(1)} %bitcast.29, bf16[2880,768]{1,0:T(8,128)(2,1)} %copy-done.3, bf16[2880,768]{1,0:T(8,128)(2,1)} %collective-permute-done.up_b_hbm, bf16[2880,768]{1,0:T(8,128)(2,1)} %copy-done.4, bf16[2880,768]{1,0:T(8,128)(2,1)} %copy-done.5), custom_call_target="tpu_custom_call" | custom-call | tf_op jit(solution)/shard_map/expert/pallas_call | solution.py:252
  93.5 0.0 copy-start
  93.6 0.0 copy-start.1
  93.6 0.0 copy-start.2
  93.6 7.6 %all-to-all-start.1 = ((bf16[128,8,1152]{2,1,0:T(8,128)(2,1)}), bf16[128,8,1152]{2,1,0:T(8,128)(2,1)}, u32[]{:S(2)}, u32[]{:S(2)}) async-start(bf16[128,8,1152]{2,1,0:T(8,128)(2,1)} %bitcast.35), calls=%async_computation.1 | async-start | bytes 4718592 | tf_op jit(solution)/shard_map/all_to_all | solution.py:329
  101.3 2.2 %mix_weights.1.weights_ref = bf16[3,512,1024]{2,1,0:T(8,128)(2,1)S(1)} custom-call(s32[1]{0:T(128)} %bitcast.h_ref, s32[2,4,64]{2,1,0:T(4,128)S(1)} %bitcast.31, s32[2,32]{1,0:T(2,128)S(1)} %bitcast.33, f32[2,4,64]{2,1,0:T(4,128)S(1)} %bitcast.34), custom_call_target="tpu_custom_call" | custom-call | tf_op jit(solution)/shard_map/mix_weights/pallas_call | solution.py:161
  103.5 53.6 %all-to-all-done.1 = bf16[128,8,1152]{2,1,0:T(8,128)(2,1)} async-done(((bf16[128,8,1152]{2,1,0:T(8,128)(2,1)}), bf16[128,8,1152]{2,1,0:T(8,128)(2,1)}, u32[]{:S(2)}, u32[]{:S(2)}) %all-to-all-start.1) | async-done | bytes 2359328 | tf_op jit(solution)/shard_map/all_to_all | solution.py:329
  157.0 4.2 %combine.1 = (bf16[2,64,1440]{2,1,0:T(8,128)(2,1)}, bf16[64,1440]{1,0:T(8,128)(2,1)S(1)}) custom-call(s32[1]{0:T(128)} %bitcast.h_ref, bf16[3,512,1024]{2,1,0:T(8,128)(2,1)S(1)} %mix_weights.1.weights_ref, bf16[1024,1152]{1,0:T(8,128)(2,1)} %bitcast.14.in_ref), custom_call_target="tpu_custom_call" | custom-call | tf_op jit(solution)/shard_map/combine/pallas_call | solution.py:296
  161.3 4.6 %collective-permute-start.2 = (bf16[64,1440]{1,0:T(8,128)(2,1)S(1)}, bf16[64,1440]{1,0:T(8,128)(2,1)S(1)}, u32[]{:S(2)}, u32[]{:S(2)}) collective-permute-start(bf16[64,1440]{1,0:T(8,128)(2,1)S(1)} %get-tuple-element.12), channel_id=1, source_target_pairs={{0,1},{1,0},{2,3},{3,2},{4,5},{5,4},{6,7},{7,6},{8,9},{9,8},{10,11... | collective-permute-start | bytes 552968 | tf_op jit(solution)/shard_map/ppermute | solution.py:333
  165.9 1.1 collective-permute-done.2.other_ref
  166.9 0.7 finish.1
  (13 shorter events, 0.0 us)
Async XLA Ops:
  0.0 20.4 %copy-start.7 = (bf16[1,24,2880]{2,1,0:T(8,128)(2,1)S(1)}, bf16[1,24,2880]{2,1,0:T(8,128)(2,1)}, u32[]{:S(2)}) copy-start(bf16[1,24,2880]{2,1,0:T(8,128)(2,1)} %param.15) | copy-start | bytes 414724
  3.6 74.6 %all-to-all-start = ((bf16[128,8,1152]{2,1,0:T(8,128)(2,1)}), bf16[128,8,1152]{2,1,0:T(8,128)(2,1)S(1)}, u32[]{:S(2)}, u32[]{:S(2)}) async-start(bf16[128,8,1152]{2,1,0:T(8,128)(2,1)} %bitcast.36), calls=%async_computation | async-start | bytes 4718592 | tf_op jit(solution)/shard_map/all_to_all | solution.py:329
  20.4 5.4 %copy-start.6 = (bf16[1,90,768]{2,1,0:T(8,128)(2,1)S(1)}, bf16[1,90,768]{2,1,0:T(8,128)(2,1)}, u32[]{:S(2)}) copy-start(bf16[1,90,768]{2,1,0:T(8,128)(2,1)} %param.13) | copy-start | bytes 414724
  24.8 4.9 %copy-start.4 = (bf16[2880,768]{1,0:T(8,128)(2,1)}, bf16[2880,768]{1,0:T(8,128)(2,1)S(1)}, u32[]{:S(2)}) copy-start(bf16[2880,768]{1,0:T(8,128)(2,1)S(1)} %fusion.1.down_a_hbm) | copy-start | bytes 13271044
  24.8 8.2 %collective-permute-start.1 = (bf16[2880,768]{1,0:T(8,128)(2,1)S(1)}, bf16[2880,768]{1,0:T(8,128)(2,1)S(1)}, u32[]{:S(2)}, u32[]{:S(2)}) collective-permute-start(bf16[2880,768]{1,0:T(8,128)(2,1)S(1)} %fusion.1.down_a_hbm), channel_id=1, source_target_pairs={{0,1},{1,0},{2,3},{3,2},{4,5},{5,4},{6,7},{7,6},{8,9},{9,8},{10,11... | collective-permute-start | bytes 13271048 | tf_op jit(solution)/shard_map/ppermute | solution.py:333
  29.6 3.3 %copy-start.3 = (bf16[2880,768]{1,0:T(8,128)(2,1)}, bf16[2880,768]{1,0:T(8,128)(2,1)S(1)}, u32[]{:S(2)}) copy-start(bf16[2880,768]{1,0:T(8,128)(2,1)S(1)} %fusion.2.up_a_hbm) | copy-start | bytes 13271044
  29.7 9.7 %collective-permute-start = (bf16[2880,768]{1,0:T(8,128)(2,1)S(1)}, bf16[2880,768]{1,0:T(8,128)(2,1)}, u32[]{:S(2)}, u32[]{:S(2)}) collective-permute-start(bf16[2880,768]{1,0:T(8,128)(2,1)S(1)} %fusion.2.up_a_hbm), channel_id=1, source_target_pairs={{0,1},{1,0},{2,3},{3,2},{4,5},{5,4},{6,7},{7,6},{8,9},{9,8},{10,11... | collective-permute-start | bytes 13271048 | tf_op jit(solution)/shard_map/ppermute | solution.py:333
  32.9 2.0 %copy-start.5 = (bf16[2880,768]{1,0:T(8,128)(2,1)}, bf16[2880,768]{1,0:T(8,128)(2,1)S(1)}, u32[]{:S(2)}) copy-start(bf16[2880,768]{1,0:T(8,128)(2,1)S(1)} %collective-permute-done.1.down_b_hbm) | copy-start | bytes 13271044
  93.5 7.7 %copy-start = (s32[2,64,4]{1,2,0:T(4,128)S(1)}, s32[2,64,4]{1,2,0:T(4,128)}, u32[]{:S(2)}) copy-start(s32[2,64,4]{1,2,0:T(4,128)} %param.9) | copy-start | bytes 6148
  93.6 7.7 %copy-start.1 = (s32[32,2]{0,1:T(2,128)S(1)}, s32[32,2]{0,1:T(2,128)}, u32[]{:S(2)}) copy-start(s32[32,2]{0,1:T(2,128)} %param.11) | copy-start | bytes 772
  93.6 7.7 %copy-start.2 = (f32[2,64,4]{1,2,0:T(4,128)S(1)}, f32[2,64,4]{1,2,0:T(4,128)}, u32[]{:S(2)}) copy-start(f32[2,64,4]{1,2,0:T(4,128)} %param.10) | copy-start | bytes 6148
  93.6 63.5 %all-to-all-start.1 = ((bf16[128,8,1152]{2,1,0:T(8,128)(2,1)}), bf16[128,8,1152]{2,1,0:T(8,128)(2,1)}, u32[]{:S(2)}, u32[]{:S(2)}) async-start(bf16[128,8,1152]{2,1,0:T(8,128)(2,1)} %bitcast.35), calls=%async_computation.1 | async-start | bytes 4718592 | tf_op jit(solution)/shard_map/all_to_all | solution.py:329
  161.3 5.7 %collective-permute-start.2 = (bf16[64,1440]{1,0:T(8,128)(2,1)S(1)}, bf16[64,1440]{1,0:T(8,128)(2,1)S(1)}, u32[]{:S(2)}, u32[]{:S(2)}) collective-permute-start(bf16[64,1440]{1,0:T(8,128)(2,1)S(1)} %get-tuple-element.12), channel_id=1, source_target_pairs={{0,1},{1,0},{2,3},{3,2},{4,5},{5,4},{6,7},{7,6},{8,9},{9,8},{10,11... | collective-permute-start | bytes 552968 | tf_op jit(solution)/shard_map/ppermute | solution.py:333

commit v3 on v2

--- a/solution.py
+++ b/solution.py
@@ -15,7 +15,7 @@
 LANES = 1152
 THIRD = 384
 WIDE = 1536
-CHUNK = 256
+CHUNK = 384
 BF = jnp.bfloat16
 F32 = jnp.float32
 
@@ -47,11 +47,15 @@
     return (moved * hf + eye * (1.0 - hf * named)).astype(BF)
 
 
-def slot_codes(place, ids):
+def owners(ids):
     owner = jnp.zeros((E, TOK), F32)
     for k in range(TOP):
         owner = owner + one_hot(ids[k : k + 1, :] == iota((E, TOK), 0), F32)
-    named = dot(place, owner.astype(BF)).astype(BF)
+    return owner.astype(BF)
+
+
+def slot_codes(place, ids):
+    named = dot(place, owners(ids)).astype(BF)
     earlier = one_hot(iota((TOK, TOK), 0) < iota((TOK, TOK), 1))
     rank = dot(named, earlier)
     return (named.astype(F32) * (rank + 1.0)).astype(BF)
@@ -74,10 +78,13 @@
     zero_ref[...] = jnp.zeros(zero_ref.shape, BF)
     for copy in small:
         copy.wait()
-    codes = slot_codes(placement(h, mig[...]), ids[...])
-    repeat = one_hot((iota((TOK, 4 * TOK), 1) & (TOK - 1)) == iota((TOK, 4 * TOK), 0))
+    owner = owners(ids[...])
+    column = iota((TOK, 4 * TOK), 1) & (TOK - 1)
+    token = iota((TOK, 4 * TOK), 0)
+    codes = dot(owner, one_hot(token == column)) * (dot(owner, one_hot(token < column)) + 1.0)
     spread = one_hot((iota((E * SUB, E), 0) >> 3) == iota((E * SUB, E), 1))
-    codes = dot(spread, dot(codes, repeat).astype(BF)).reshape(E, SUB, 4 * TOK)
+    spread = dot(spread, placement(h, mig[...])).astype(BF)
+    codes = dot(spread, codes.astype(BF)).reshape(E, SUB, 4 * TOK)
     p = iota((SUB, 4 * TOK), 0)
     b = iota((SUB, 4 * TOK), 1) >> 6
     load.wait()
@@ -138,8 +145,6 @@
     gate = jnp.zeros((E, TOK), F32)
     for k in range(TOP):
         gate = gate + jnp.where(ids[k : k + 1, :] == iota((E, TOK), 0), gates[k : k + 1, :], 0.0)
-    high = gate.astype(BF)
-    low = (gate - high.astype(F32)).astype(BF)
     repeat = one_hot((iota((4 * TOK, TOK), 0) & (TOK - 1)) == iota((4 * TOK, TOK), 1))
     spread = one_hot((iota((E, E * SUB), 1) >> 3) == iota((E, E * SUB), 0))
 
@@ -147,14 +152,14 @@
         return dot(dot(repeat, x, 1, 1).astype(BF), spread)
 
     codes = widened(codes)
-    high = widened(dot(place, high).astype(BF))
-    low = widened(dot(place, low).astype(BF))
+    gate = widened(dot(place, gate.astype(BF)).astype(BF))
     p = iota((4 * TOK, E * SUB), 1) & (SUB - 1)
     b = iota((4 * TOK, E * SUB), 0) >> 6
     for i in range(3):
-        hit = codes == wanted(p, b, i)
-        out_ref[i, 0 : 4 * TOK, :] = jnp.where(hit, high, 0.0).astype(BF)
-        out_ref[i, 4 * TOK : 8 * TOK, :] = jnp.where(hit, low, 0.0).astype(BF)
+        part = jnp.where(codes == wanted(p, b, i), gate, 0.0).astype(BF)
+        if i == 0:
+            out_ref[3] = part[0 : 2 * TOK]
+        out_ref[i] = part[2 * TOK : 4 * TOK]
 
 
 def mix_weights(h, ids, mig, gates):
@@ -162,7 +167,7 @@
         mix_body,
         in_specs=[SMEM, VMEM, VMEM, VMEM],
         out_specs=VMEM,
-        out_shape=jax.ShapeDtypeStruct((3, 8 * TOK, E * SUB), BF),
+        out_shape=jax.ShapeDtypeStruct((4, 2 * TOK, E * SUB), BF),
         name="mix_weights",
         compiler_params=pltpu.CompilerParams(vmem_limit_bytes=24 << 20),
     )(h, ids, mig, gates)
@@ -199,7 +204,7 @@
         for c in range(HW2 // CHUNK):
             ups[n * (HW2 // CHUNK) + c].wait()
             pre = dot(rows[:, 0:D], up_ref[:, c * CHUNK : (c + 1) * CHUNK])
-            act = pre / (1.0 + jnp.exp(-1.702 * pre))
+            act = pre * (0.5 + 0.5 * jnp.tanh(0.851 * pre))
             hidden[:, n * HW2 + c * CHUNK : n * HW2 + (c + 1) * CHUNK] = act.astype(BF)
 
     for load in downs:
@@ -271,8 +276,8 @@
     h = h_ref[0]
     mains, tail = [], 0.0
     for i in range(3):
-        out = dot(weights_ref[i], in_ref[:, i * THIRD : (i + 1) * THIRD])
-        out = out[0 : 4 * TOK] + out[4 * TOK : 8 * TOK]
+        pair = jnp.concatenate([weights_ref[3], weights_ref[i]], axis=0)
+        out = dot(pair, in_ref[:, i * THIRD : (i + 1) * THIRD])
         mains.append(out[0 : 2 * TOK])
         tail = tail + out[2 * TOK : 4 * TOK]
     for g in range(2):

time: 168 us -> 163 us (0.970)
  Pallas kernels: 26 us -> 20.2 us
  waiting for transfers between devices: 100 us -> 104 us
  other arithmetic: 3.82 us -> 1.72 us
    ppermute x3, waiting for transfers between devices: 7.79 us -> 10.6 us  [swapped(): return lax.ppermute(x, 'pair', [(0, 1), (1, 0)])]
    pallas_call x1, Pallas kernels: 4.24 us -> 1.78 us  [combine(): pl.pallas_call(combine_body, in_specs=[SMEM, VMEM, VMEM], out_specs=[VMEM...]
    pallas_call x1, Pallas kernels: 15.3 us -> 12.9 us  [expert(): pl.pallas_call(expert_body, in_specs=[VMEM, HBM, HBM, HBM, HBM], out_spec...]
    convert_element_type x1, other arithmetic: 3.09 us -> 1 us  [dequantize_up(): return shaped.astype(BF).reshape(D, HW2)]
  transfers between devices with their start and end apart: 5 -> 5, of which waited for: 5 -> 5; matrix products, arithmetic and copies ran while one was open for 5% -> 4% of each run, Pallas kernels for 1% -> 1%
where the time goes in v3:
time: 163 us; the launch traced here: 162 us
  waiting for transfers between devices  104 us (64%)
  starting transfers between devices  29 us (18%)
  Pallas kernels  20.2 us (12%)
  matrix products  4.63 us (3%)
  local copies, waits for them, and re-layouts  2.57 us (2%)
  other arithmetic  1.72 us (1%)
    all_to_all x2, waiting for transfers between devices, exchange(): lax.all_to_all(blocks, ('col', 'row'), 0, 0, tiled=True)  93.2 us
    all_to_all x2, starting transfers between devices, exchange(): lax.all_to_all(blocks, ('col', 'row'), 0, 0, tiled=True)  23.1 us
    pallas_call x1, Pallas kernels, expert(): pl.pallas_call(expert_body, in_specs=[VMEM, HBM, HBM, HBM, HBM], out_spec...  12.9 us
    ppermute x3, waiting for transfers between devices, swapped(): return lax.ppermute(x, 'pair', [(0, 1), (1, 0)])  10.6 us
    ppermute x3, starting transfers between devices, swapped(): return lax.ppermute(x, 'pair', [(0, 1), (1, 0)])  5.91 us
    dot_general x1, matrix products, dequantize_down(): spread = jnp.einsum('bn,bk->nk', scales, group, preferred_element_type=F32)  4.63 us
    pallas_call x1, Pallas kernels, pack(): pl.pallas_call(pack_body, in_specs=[SMEM, HBM, HBM, HBM], out_specs=[HBM,...  3.39 us
  transfers between devices with their start and end apart: 5, of which 5 were waited for; matrix products, arithmetic and copies ran while one was open for 4% of the time, Pallas kernels for 1%

profile of v3, /device:TPU:1, one launch (start us, length us, event | category | flops | bytes accessed | tf_op | source)
XLA Modules:
  0.0 162.2 jit_solution(615510564645096997)
XLA Ops:
  0.0 3.4 %pack.1 = (bf16[1024,1152]{1,0:T(8,128)(2,1)}, bf16[16,128]{1,0:T(8,128)(2,1)S(1)}) custom-call(s32[1]{0:T(128)} %bitcast.h_ref, s32[2,4,64]{2,1,0:T(4,128)} %bitcast.31, s32[2,32]{1,0:T(2,128)} %bitcast.34, bf16[2,64,2880]{2,1,0:T(8,128)(2,1)} %tok_ref.1), custom_call_target="tpu_custom_call" | custom-call | tf_op jit(solution)/shard_map/pack/pallas_call | solution.py:119
  3.4 0.0 slice-start
  3.4 16.5 %all-to-all-start = ((bf16[128,8,1152]{2,1,0:T(8,128)(2,1)}), bf16[128,8,1152]{2,1,0:T(8,128)(2,1)S(1)}, u32[]{:S(2)}, u32[]{:S(2)}) async-start(bf16[128,8,1152]{2,1,0:T(8,128)(2,1)} %bitcast.39), calls=%async_computation | async-start | bytes 4718592 | tf_op jit(solution)/shard_map/all_to_all | solution.py:334
  19.9 0.5 slice.4
  20.4 4.6 %fusion.1.down_a_hbm = bf16[2880,768]{1,0:T(8,128)(2,1)S(1)} fusion(bf16[1,768,2880]{1,2,0:T(8,128)(2,1)} %param.14, bf16[1,24,2880]{2,1,0:T(8,128)(2,1)S(1)} %copy-done.7, bf16[]{:T(256)} %bitcast.7, s32[768]{0:T(1024)S(1)} %get-tuple-element.13, s32[768]{0:T(1024)S(1)} %get-tuple-element.14, pred[768]{0:T(1024)(128)(4,1)S(1)} %fusion.11), kind=kOutput, calls=%fused_computation.2 | convolution fusion | flops 112909824 | bytes 8992514 | tf_op jit(solution)/shard_map/bn,bk->nk/dot_general | solution.py:348
  25.1 1.0 collective-permute-start.1
  26.1 0.7 bitcast_convert_fusion
  26.9 1.0 fusion.2.up_a_hbm
  27.9 0.3 collective-permute-start
  28.2 5.1 %collective-permute-done.1.down_b_hbm = bf16[2880,768]{1,0:T(8,128)(2,1)S(1)} collective-permute-done((bf16[2880,768]{1,0:T(8,128)(2,1)S(1)}, bf16[2880,768]{1,0:T(8,128)(2,1)S(1)}, u32[]{:S(2)}, u32[]{:S(2)}) %collective-permute-start.1) | collective-permute-done | bytes 4423712 | tf_op jit(solution)/shard_map/ppermute | solution.py:338
  33.3 2.0 %copy-done.5 = bf16[2880,768]{1,0:T(8,128)(2,1)} copy-done((bf16[2880,768]{1,0:T(8,128)(2,1)}, bf16[2880,768]{1,0:T(8,128)(2,1)S(1)}, u32[]{:S(2)}) %copy-start.5) | copy-done | bytes 4423704
  35.3 4.4 %collective-permute-done.up_b_hbm = bf16[2880,768]{1,0:T(8,128)(2,1)} collective-permute-done((bf16[2880,768]{1,0:T(8,128)(2,1)S(1)}, bf16[2880,768]{1,0:T(8,128)(2,1)}, u32[]{:S(2)}, u32[]{:S(2)}) %collective-permute-start) | collective-permute-done | bytes 4423712 | tf_op jit(solution)/shard_map/ppermute | solution.py:338
  39.7 38.5 %all-to-all-done = bf16[128,8,1152]{2,1,0:T(8,128)(2,1)S(1)} async-done(((bf16[128,8,1152]{2,1,0:T(8,128)(2,1)}), bf16[128,8,1152]{2,1,0:T(8,128)(2,1)S(1)}, u32[]{:S(2)}, u32[]{:S(2)}) %all-to-all-start) | async-done | bytes 2359328 | tf_op jit(solution)/shard_map/all_to_all | solution.py:334
  78.2 12.9 %expert.1 = bf16[1024,1152]{1,0:T(8,128)(2,1)} custom-call(bf16[1024,1152]{1,0:T(8,128)(2,1)S(1)} %bitcast.30, bf16[2880,768]{1,0:T(8,128)(2,1)} %copy-done.3, bf16[2880,768]{1,0:T(8,128)(2,1)} %collective-permute-done.up_b_hbm, bf16[2880,768]{1,0:T(8,128)(2,1)} %copy-done.4, bf16[2880,768]{1,0:T(8,128)(2,1)} %copy-done.5), custom_call_target="tpu_custom_call" | custom-call | tf_op jit(solution)/shard_map/expert/pallas_call | solution.py:257
  91.1 0.0 copy-start
  91.1 0.0 copy-start.1
  91.2 0.0 copy-start.2
  91.2 6.6 %all-to-all-start.1 = ((bf16[128,8,1152]{2,1,0:T(8,128)(2,1)}), bf16[128,8,1152]{2,1,0:T(8,128)(2,1)S(1)}, u32[]{:S(2)}, u32[]{:S(2)}) async-start(bf16[128,8,1152]{2,1,0:T(8,128)(2,1)} %bitcast.36), calls=%async_computation.1 | async-start | bytes 4718592 | tf_op jit(solution)/shard_map/all_to_all | solution.py:334
  97.8 1.5 mix_weights.1.weights_ref
  99.3 54.7 %all-to-all-done.1 = bf16[128,8,1152]{2,1,0:T(8,128)(2,1)S(1)} async-done(((bf16[128,8,1152]{2,1,0:T(8,128)(2,1)}), bf16[128,8,1152]{2,1,0:T(8,128)(2,1)S(1)}, u32[]{:S(2)}, u32[]{:S(2)}) %all-to-all-start.1) | async-done | bytes 2359328 | tf_op jit(solution)/shard_map/all_to_all | solution.py:334
  153.9 1.8 %combine.1 = (bf16[2,64,1440]{2,1,0:T(8,128)(2,1)}, bf16[64,1440]{1,0:T(8,128)(2,1)S(1)}) custom-call(s32[1]{0:T(128)} %bitcast.h_ref, bf16[4,128,1024]{2,1,0:T(8,128)(2,1)S(1)} %mix_weights.1.weights_ref, bf16[1024,1152]{1,0:T(8,128)(2,1)S(1)} %bitcast.29), custom_call_target="tpu_custom_call" | custom-call | tf_op jit(solution)/shard_map/combine/pallas_call | solution.py:301
  155.7 4.6 %collective-permute-start.2 = (bf16[64,1440]{1,0:T(8,128)(2,1)S(1)}, bf16[64,1440]{1,0:T(8,128)(2,1)S(1)}, u32[]{:S(2)}, u32[]{:S(2)}) collective-permute-start(bf16[64,1440]{1,0:T(8,128)(2,1)S(1)} %get-tuple-element.12), channel_id=1, source_target_pairs={{0,1},{1,0},{2,3},{3,2},{4,5},{5,4},{6,7},{7,6},{8,9},{9,8},{10,11... | collective-permute-start | bytes 552968 | tf_op jit(solution)/shard_map/ppermute | solution.py:338
  160.3 1.1 collective-permute-done.2.other_ref
  161.3 0.7 finish.1
  (18 shorter events, 0.0 us)
Async XLA Ops:
  0.0 20.4 %copy-start.7 = (bf16[1,24,2880]{2,1,0:T(8,128)(2,1)S(1)}, bf16[1,24,2880]{2,1,0:T(8,128)(2,1)}, u32[]{:S(2)}) copy-start(bf16[1,24,2880]{2,1,0:T(8,128)(2,1)} %param.15) | copy-start | bytes 414724
  3.4 23.5 %slice-start = ((s8[4423680]{0:T(1024)(128)(4,1)}), s8[229376]{0:T(1024)(128)(4,1)S(1)}, s32[]{:S(2)}) async-start(s8[4423680]{0:T(1024)(128)(4,1)} %bitcast.37), calls=%async_computation.2 | async-start | bytes 458752
  3.4 74.8 %all-to-all-start = ((bf16[128,8,1152]{2,1,0:T(8,128)(2,1)}), bf16[128,8,1152]{2,1,0:T(8,128)(2,1)S(1)}, u32[]{:S(2)}, u32[]{:S(2)}) async-start(bf16[128,8,1152]{2,1,0:T(8,128)(2,1)} %bitcast.39), calls=%async_computation | async-start | bytes 4718592 | tf_op jit(solution)/shard_map/all_to_all | solution.py:334
  20.4 5.7 %copy-start.6 = (bf16[1,90,768]{2,1,0:T(8,128)(2,1)S(1)}, bf16[1,90,768]{2,1,0:T(8,128)(2,1)}, u32[]{:S(2)}) copy-start(bf16[1,90,768]{2,1,0:T(8,128)(2,1)} %param.13) | copy-start | bytes 414724
  20.4 6.4 %slice-start.1 = ((s8[4423680]{0:T(1024)(128)(4,1)}), s8[4194304]{0:T(1024)(128)(4,1)S(1)}, s32[]{:S(2)}) async-start(s8[4423680]{0:T(1024)(128)(4,1)} %bitcast.37), calls=%async_computation.3 | async-start | bytes 8388608
  25.1 2.8 %copy-start.4 = (bf16[2880,768]{1,0:T(8,128)(2,1)}, bf16[2880,768]{1,0:T(8,128)(2,1)S(1)}, u32[]{:S(2)}) copy-start(bf16[2880,768]{1,0:T(8,128)(2,1)S(1)} %fusion.1.down_a_hbm) | copy-start | bytes 13271044
  25.1 8.2 %collective-permute-start.1 = (bf16[2880,768]{1,0:T(8,128)(2,1)S(1)}, bf16[2880,768]{1,0:T(8,128)(2,1)S(1)}, u32[]{:S(2)}, u32[]{:S(2)}) collective-permute-start(bf16[2880,768]{1,0:T(8,128)(2,1)S(1)} %fusion.1.down_a_hbm), channel_id=1, source_target_pairs={{0,1},{1,0},{2,3},{3,2},{4,5},{5,4},{6,7},{7,6},{8,9},{9,8},{10,11... | collective-permute-start | bytes 13271048 | tf_op jit(solution)/shard_map/ppermute | solution.py:338
  27.9 5.4 %copy-start.3 = (bf16[2880,768]{1,0:T(8,128)(2,1)}, bf16[2880,768]{1,0:T(8,128)(2,1)S(1)}, u32[]{:S(2)}) copy-start(bf16[2880,768]{1,0:T(8,128)(2,1)S(1)} %fusion.2.up_a_hbm) | copy-start | bytes 13271044
  27.9 11.8 %collective-permute-start = (bf16[2880,768]{1,0:T(8,128)(2,1)S(1)}, bf16[2880,768]{1,0:T(8,128)(2,1)}, u32[]{:S(2)}, u32[]{:S(2)}) collective-permute-start(bf16[2880,768]{1,0:T(8,128)(2,1)S(1)} %fusion.2.up_a_hbm), channel_id=1, source_target_pairs={{0,1},{1,0},{2,3},{3,2},{4,5},{5,4},{6,7},{7,6},{8,9},{9,8},{10,11... | collective-permute-start | bytes 13271048 | tf_op jit(solution)/shard_map/ppermute | solution.py:338
  33.3 2.0 %copy-start.5 = (bf16[2880,768]{1,0:T(8,128)(2,1)}, bf16[2880,768]{1,0:T(8,128)(2,1)S(1)}, u32[]{:S(2)}) copy-start(bf16[2880,768]{1,0:T(8,128)(2,1)S(1)} %collective-permute-done.1.down_b_hbm) | copy-start | bytes 13271044
  91.1 6.6 %copy-start = (s32[2,64,4]{1,2,0:T(4,128)S(1)}, s32[2,64,4]{1,2,0:T(4,128)}, u32[]{:S(2)}) copy-start(s32[2,64,4]{1,2,0:T(4,128)} %param.9) | copy-start | bytes 6148
  91.1 6.6 %copy-start.1 = (f32[2,64,4]{1,2,0:T(4,128)S(1)}, f32[2,64,4]{1,2,0:T(4,128)}, u32[]{:S(2)}) copy-start(f32[2,64,4]{1,2,0:T(4,128)} %param.10) | copy-start | bytes 6148
  91.2 6.6 %copy-start.2 = (s32[32,2]{0,1:T(2,128)S(1)}, s32[32,2]{0,1:T(2,128)}, u32[]{:S(2)}) copy-start(s32[32,2]{0,1:T(2,128)} %param.11) | copy-start | bytes 772
  91.2 62.8 %all-to-all-start.1 = ((bf16[128,8,1152]{2,1,0:T(8,128)(2,1)}), bf16[128,8,1152]{2,1,0:T(8,128)(2,1)S(1)}, u32[]{:S(2)}, u32[]{:S(2)}) async-start(bf16[128,8,1152]{2,1,0:T(8,128)(2,1)} %bitcast.36), calls=%async_computation.1 | async-start | bytes 4718592 | tf_op jit(solution)/shard_map/all_to_all | solution.py:334
  155.7 5.7 %collective-permute-start.2 = (bf16[64,1440]{1,0:T(8,128)(2,1)S(1)}, bf16[64,1440]{1,0:T(8,128)(2,1)S(1)}, u32[]{:S(2)}, u32[]{:S(2)}) collective-permute-start(bf16[64,1440]{1,0:T(8,128)(2,1)S(1)} %get-tuple-element.12), channel_id=1, source_target_pairs={{0,1},{1,0},{2,3},{3,2},{4,5},{5,4},{6,7},{7,6},{8,9},{9,8},{10,11... | collective-permute-start | bytes 552968 | tf_op jit(solution)/shard_map/ppermute | solution.py:338

commit v4 on v3

--- a/solution.py
+++ b/solution.py
@@ -4,6 +4,7 @@
 from jax.experimental import pallas as pl
 from jax.experimental.pallas import tpu as pltpu
 from jax.sharding import PartitionSpec as P
+
 
 D = 2880
 HALF = D // 2
@@ -14,7 +15,8 @@
 SUB = 8
 LANES = 1152
 THIRD = 384
-WIDE = 1536
+MAIN = 2176
+GROUPS = 640
 CHUNK = 384
 BF = jnp.bfloat16
 F32 = jnp.float32
@@ -65,7 +67,7 @@
     return ref.at[:, i * THIRD : (i + 1) * THIRD]
 
 
-def pack_body(h_ref, ids_ref, mig_ref, tok_ref, out_ref, zero_ref, tok, tail, rows, ids, mig, sems):
+def pack_body(h_ref, ids_ref, mig_ref, tok_ref, out_ref, zero_ref, tok, source, rows, ids, mig, sems):
     h = h_ref[0]
     small = [
         pltpu.make_async_copy(ids_ref.at[h], ids, sems.at[4]),
@@ -76,36 +78,37 @@
     load = pltpu.make_async_copy(tok_ref.at[h], tok, sems.at[3])
     load.start()
     zero_ref[...] = jnp.zeros(zero_ref.shape, BF)
+    source[TOK:, :] = jnp.zeros((3 * TOK, MAIN), BF)
     for copy in small:
         copy.wait()
     owner = owners(ids[...])
     column = iota((TOK, 4 * TOK), 1) & (TOK - 1)
     token = iota((TOK, 4 * TOK), 0)
     codes = dot(owner, one_hot(token == column)) * (dot(owner, one_hot(token < column)) + 1.0)
-    spread = one_hot((iota((E * SUB, E), 0) >> 3) == iota((E * SUB, E), 1))
+    spread = one_hot((iota((E * 4, E), 0) >> 2) == iota((E * 4, E), 1))
     spread = dot(spread, placement(h, mig[...])).astype(BF)
-    codes = dot(spread, codes.astype(BF)).reshape(E, SUB, 4 * TOK)
-    p = iota((SUB, 4 * TOK), 0)
+    codes = dot(spread, codes.astype(BF)).reshape(E // 2, SUB, 4 * TOK)
+    q = iota((SUB, 4 * TOK), 0) & 3
     b = iota((SUB, 4 * TOK), 1) >> 6
+    want = jnp.where(q < 3, jnp.where(b == 0, q + 1, -1), jnp.where(b > 0, b, -1)).astype(F32)
+    select = one_hot(codes == want[None]).reshape(E * 4, 4 * TOK)
     load.wait()
-    left = D - WIDE - LANES
-    tail[:, 0:left] = tok[:, WIDE + LANES : D]
-    tail[:, left:THIRD] = jnp.zeros((TOK, THIRD - left), BF)
+    source[0:TOK, :] = tok[:, 0:MAIN]
+    piece = tok[:, MAIN + GROUPS : D]
+    for j in range(3):
+        mine = slice((j + 1) * TOK, (j + 2) * TOK)
+        source[mine, j * GROUPS : (j + 1) * GROUPS] = tok[:, MAIN : MAIN + GROUPS]
+    source[TOK : 2 * TOK, 3 * GROUPS : 3 * GROUPS + 64] = piece
+    shifted = jnp.concatenate([jnp.zeros((TOK, 64), F32), piece.astype(F32)], axis=1)
+    source[2 * TOK : 3 * TOK, 3 * GROUPS : 3 * GROUPS + 128] = shifted.astype(BF)
+    source[3 * TOK : 4 * TOK, 3 * GROUPS + 128 : 3 * GROUPS + 192] = piece
     stores = []
-    for i in range(3):
-        select = one_hot(codes == wanted(p, b, i)[None]).reshape(E * SUB, 4 * TOK)
-        source = jnp.concatenate(
-            [
-                tok[:, i * THIRD : (i + 1) * THIRD],
-                tok[:, WIDE + i * THIRD : WIDE + (i + 1) * THIRD],
-                tok[:, LANES:WIDE],
-                tail[...],
-            ],
-            axis=0,
-        )
-        rows[:, i * THIRD : (i + 1) * THIRD] = dot(select, source).astype(BF)
-        stores.append(pltpu.make_async_copy(third(rows, i), third(out_ref, i), sems.at[i]))
-        stores[i].start()
+    for n, (c0, c1) in enumerate(((0, 768), (768, 1536), (1536, MAIN))):
+        part = dot(select, source[:, c0:c1]).astype(BF)
+        rows[:, :, c0:c1] = part.reshape(E, 4, c1 - c0)
+        cut = (slice(None), slice(None), pl.ds(c0, c1 - c0))
+        stores.append(pltpu.make_async_copy(rows.at[cut], out_ref.at[cut], sems.at[n]))
+        stores[n].start()
     for store in stores:
         store.wait()
 
@@ -122,14 +125,14 @@
         out_specs=[HBM, VMEM],
         scratch_shapes=[
             pltpu.VMEM((TOK, D), BF),
-            pltpu.VMEM((TOK, THIRD), BF),
-            pltpu.VMEM((E * SUB, LANES), BF),
+            pltpu.VMEM((4 * TOK, MAIN), BF),
+            pltpu.VMEM((E, 4, MAIN), BF),
             pltpu.VMEM((TOP, TOK), jnp.int32),
             pltpu.VMEM(mig.shape, jnp.int32),
             pltpu.SemaphoreType.DMA((6,)),
         ],
         out_shape=[
-            pltpu.HBM((E * SUB, LANES), BF),
+            pltpu.HBM((E, 4, MAIN), BF),
             jax.ShapeDtypeStruct((16, 128), BF),
         ],
         name="pack",
@@ -173,22 +176,12 @@
     )(h, ids, mig, gates)
 
 
-def pieces():
-    for q in range(6):
-        j, g = q // 2, q % 2
-        for part in range(WIDE // 128):
-            if part < 9:
-                yield j, g * WIDE + part * 128, part, q
-            else:
-                yield j, g * WIDE + part * 128, 3 * (q % 3) + part - 9, 6 + q // 3
-
-
 def expert_body(
     in_ref, up_a_hbm, up_b_hbm, down_a_hbm, down_b_hbm, out_hbm,
-    wide, rows, hidden, out_ref, up_a, up_b, down_a, down_b, up_sems, down_sems, out_sems,
+    wide, wide_in, rows, hidden, out_ref, up_a, up_b, down_a, down_b, up_sems, down_sems, out_sems,
 ):
     ups, downs, stores = [], [], []
-    for n, (src, dst) in enumerate(((up_a_hbm, up_a), (up_b_hbm, up_b))):
+    for src, dst in ((up_a_hbm, up_a), (up_b_hbm, up_b)):
         for c in range(HW2 // CHUNK):
             cut = (slice(None), pl.ds(c * CHUNK, CHUNK))
             ups.append(pltpu.make_async_copy(src.at[cut], dst.at[cut], up_sems.at[len(ups)]))
@@ -196,10 +189,21 @@
         downs.append(pltpu.make_async_copy(src, dst, down_sems.at[n]))
     for load in ups + downs:
         load.start()
-    for part in range(LANES // 128):
-        wide[part] = in_ref[:, part * 128 : (part + 1) * 128].astype(F32)
-    for j, lane, part, p in pieces():
-        rows[j * E : (j + 1) * E, lane : lane + 128] = wide[part, pl.ds(p, E, stride=SUB), :].astype(BF)
+    for part in range(MAIN // 128):
+        lanes = in_ref[:, :, part * 128 : (part + 1) * 128].astype(F32)
+        wide_in[part] = lanes.reshape(4 * E, 128)
+    last = MAIN // 128 - 2
+    halves = ((last, 0), (last, 64), (last + 1, 0))
+    for j in range(3):
+        mine = slice(j * E, (j + 1) * E)
+        for part in range(MAIN // 128):
+            rows[mine, part * 128 : (part + 1) * 128] = wide_in[part, pl.ds(j, E, stride=4), :].astype(BF)
+        for part in range(GROUPS // 128):
+            lane = MAIN + part * 128
+            found = wide_in[j * (GROUPS // 128) + part, pl.ds(3, E, stride=4), :]
+            rows[mine, lane : lane + 128] = found.astype(BF)
+        part, lane = halves[j]
+        rows[mine, MAIN + GROUPS : D] = wide_in[part, pl.ds(3, E, stride=4), :][:, lane : lane + 64].astype(BF)
     for n, up_ref in enumerate((up_a, up_b)):
         for c in range(HW2 // CHUNK):
             ups[n * (HW2 // CHUNK) + c].wait()
@@ -260,7 +264,8 @@
         out_specs=HBM,
         scratch_shapes=[
             pltpu.VMEM((LANES // 128, E * SUB, 128), F32),
-            pltpu.VMEM((3 * E, 2 * WIDE), BF),
+            pltpu.VMEM((MAIN // 128, 4 * E, 128), F32),
+            pltpu.VMEM((3 * E, D), BF),
             pltpu.VMEM((3 * E, 2 * HW2), BF),
             pltpu.VMEM((E * SUB, LANES), BF),
         ]
@@ -329,9 +334,8 @@
     )(h, full, on_chip(other))
 
 
-def exchange(x):
-    blocks = x.reshape(E, SUB, LANES)
-    return lax.all_to_all(blocks, ("col", "row"), 0, 0, tiled=True).reshape(E * SUB, LANES)
+def exchange(blocks):
+    return lax.all_to_all(blocks, ("col", "row"), 0, 0, tiled=True)
 
 
 def swapped(x):
@@ -364,7 +368,8 @@
     up_b = swapped(up_a)
     down_b = swapped(down_a)
     weights = mix_weights(h, ids, mig, gates)
-    returned = exchange(expert(received, up_a, up_b, down_a, down_b))
+    results = expert(received, up_a, up_b, down_a, down_b).reshape(E, SUB, LANES)
+    returned = exchange(results).reshape(E * SUB, LANES)
     full, send = combine(h, weights, returned)
     return finish(h, full, swapped(send))
 

time: 163 us -> 172 us (1.055)
  blocking collectives: 0 us -> 69.4 us
  waiting for transfers between devices: 104 us -> 56.2 us
  starting transfers between devices: 29 us -> 14.4 us
  local copies, waits for them, and re-layouts: 2.57 us -> 4.68 us
    all_to_all x0 -> x1, blocking collectives: none -> 69.4 us  [exchange(): return lax.all_to_all(blocks, ('col', 'row'), 0, 0, tiled=True)]
    all_to_all x2 -> x1, waiting for transfers between devices: 93.2 us -> 55.1 us  [exchange(): return lax.all_to_all(blocks, ('col', 'row'), 0, 0, tiled=True)]
    all_to_all x2 -> x1, starting transfers between devices: 23.1 us -> 6.36 us  [exchange(): return lax.all_to_all(blocks, ('col', 'row'), 0, 0, tiled=True)]
    ppermute x3, waiting for transfers between devices: 10.6 us -> 1.08 us  [swapped(): return lax.ppermute(x, 'pair', [(0, 1), (1, 0)])]
    ppermute x3, starting transfers between devices: 5.91 us -> 8.08 us  [swapped(): return lax.ppermute(x, 'pair', [(0, 1), (1, 0)])]
    unnamed x20, local copies, waits for them, and re-layouts: 2.06 us -> 4.17 us
  transfers between devices with their start and end apart: 5 -> 4, of which waited for: 5 -> 2; matrix products, arithmetic and copies ran while one was open for 4% -> 1% of each run, Pallas kernels for 1% -> 1%
where the time goes in v4:
time: 172 us; the launch traced here: 171 us
  blocking collectives  69.4 us (40%)
  waiting for transfers between devices  56.2 us (33%)
  Pallas kernels  20.3 us (12%)
  starting transfers between devices  14.4 us (8%)
  local copies, waits for them, and re-layouts  4.68 us (3%)
  matrix products  4.39 us (3%)
    all_to_all x1, blocking collectives, exchange(): return lax.all_to_all(blocks, ('col', 'row'), 0, 0, tiled=True)  69.4 us
    all_to_all x1, waiting for transfers between devices, exchange(): return lax.all_to_all(blocks, ('col', 'row'), 0, 0, tiled=True)  55.1 us
    pallas_call x1, Pallas kernels, expert(): pl.pallas_call(expert_body, in_specs=[VMEM, HBM, HBM, HBM, HBM], out_spec...  13 us
    ppermute x3, starting transfers between devices, swapped(): return lax.ppermute(x, 'pair', [(0, 1), (1, 0)])  8.08 us
    all_to_all x1, starting transfers between devices, exchange(): return lax.all_to_all(blocks, ('col', 'row'), 0, 0, tiled=True)  6.36 us
    dot_general x1, matrix products, dequantize_down(): spread = jnp.einsum('bn,bk->nk', scales, group, preferred_element_type=F32)  4.39 us
    unnamed x20, local copies, waits for them, and re-layouts  4.17 us
  transfers between devices with their start and end apart: 4, of which 2 were waited for; matrix products, arithmetic and copies ran while one was open for 1% of the time, Pallas kernels for 1%

profile of v4, /device:TPU:1, one launch (start us, length us, event | category | flops | bytes accessed | tf_op | source)
XLA Modules:
  0.0 171.2 jit_solution(7714253688362204879)
XLA Ops:
  0.0 0.0 slice-start
  0.0 3.4 %pack.1 = (bf16[128,4,2176]{2,1,0:T(4,128)(2,1)}, bf16[16,128]{1,0:T(8,128)(2,1)S(1)}) custom-call(s32[1]{0:T(128)} %bitcast.h_ref, s32[2,4,64]{2,1,0:T(4,128)} %bitcast.28, s32[2,32]{1,0:T(2,128)} %bitcast.31, bf16[2,64,2880]{2,1,0:T(8,128)(2,1)} %tok_ref.1), custom_call_target="tpu_custom_call" | custom-call | tf_op jit(solution)/shard_map/pack/pallas_call | solution.py:122
  3.4 0.5 slice.4
  3.9 4.4 %fusion.1.down_a_hbm = bf16[2880,768]{1,0:T(8,128)(2,1)S(1)} fusion(bf16[1,768,2880]{1,2,0:T(8,128)(2,1)} %param.14, bf16[1,24,2880]{2,1,0:T(8,128)(2,1)} %param.15, bf16[]{:T(256)} %bitcast.5, s32[768]{0:T(1024)S(1)} %get-tuple-element.13, s32[768]{0:T(1024)S(1)} %get-tuple-element.14, pred[768]{0:T(1024)(128)(4,1)S(1)} %fusion.11), kind=kOutput, calls=%fused_computation.2 | convolution fusion | flops 112909824 | bytes 8992514 | tf_op jit(solution)/shard_map/bn,bk->nk/dot_general | solution.py:352
  8.3 3.3 %collective-permute-start.1 = (bf16[2880,768]{1,0:T(8,128)(2,1)S(1)}, bf16[2880,768]{1,0:T(8,128)(2,1)S(1)}, u32[]{:S(2)}, u32[]{:S(2)}) collective-permute-start(bf16[2880,768]{1,0:T(8,128)(2,1)S(1)} %fusion.1.down_a_hbm), channel_id=1, source_target_pairs={{0,1},{1,0},{2,3},{3,2},{4,5},{5,4},{6,7},{7,6},{8,9},{9,8},{10,11... | collective-permute-start | bytes 13271048 | tf_op jit(solution)/shard_map/ppermute | solution.py:342
  11.6 0.7 bitcast_convert_fusion
  12.3 0.8 fusion.2.up_a_hbm
  13.2 0.4 collective-permute-start
  13.6 69.4 %all_to_all.10.in_ref = bf16[128,4,2176]{2,1,0:T(4,128)(2,1)S(1)} all-to-all(bf16[128,4,2176]{2,1,0:T(4,128)(2,1)} %get-tuple-element.9), channel_id=1, replica_groups=mesh['col'=16,'row'=8,'pair'=2] {'col','row'}, dimensions={0} | all-to-all | bytes 4456448 | tf_op jit(solution)/shard_map/all_to_all | solution.py:338
  83.0 0.0 collective-permute-done.1.down_b_hbm
  83.0 0.0 collective-permute-done.up_b_hbm
  83.1 2.0 %copy-done.5 = bf16[2880,768]{1,0:T(8,128)(2,1)} copy-done((bf16[2880,768]{1,0:T(8,128)(2,1)}, bf16[2880,768]{1,0:T(8,128)(2,1)S(1)}, u32[]{:S(2)}) %copy-start.5) | copy-done | bytes 4423704
  85.1 2.1 %copy-done.6 = bf16[2880,768]{1,0:T(8,128)(2,1)} copy-done((bf16[2880,768]{1,0:T(8,128)(2,1)}, bf16[2880,768]{1,0:T(8,128)(2,1)S(1)}, u32[]{:S(2)}) %copy-start.6) | copy-done | bytes 4423704
  87.2 13.0 %expert.1 = bf16[1024,1152]{1,0:T(8,128)(2,1)} custom-call(bf16[128,4,2176]{2,1,0:T(4,128)(2,1)S(1)} %all_to_all.10.in_ref, bf16[2880,768]{1,0:T(8,128)(2,1)} %copy-done.3, bf16[2880,768]{1,0:T(8,128)(2,1)} %copy-done.6, bf16[2880,768]{1,0:T(8,128)(2,1)} %copy-done.4, bf16[2880,768]{1,0:T(8,128)(2,1)} %copy-done.5), custom_call_target="tpu_custom_call" | custom-call | tf_op jit(solution)/shard_map/expert/pallas_call | solution.py:261
  100.2 0.0 copy-start
  100.2 0.0 copy-start.1
  100.2 0.0 copy-start.2
  100.2 6.4 %all-to-all-start.1 = ((bf16[128,8,1152]{2,1,0:T(8,128)(2,1)}), bf16[128,8,1152]{2,1,0:T(8,128)(2,1)S(1)}, u32[]{:S(2)}, u32[]{:S(2)}) async-start(bf16[128,8,1152]{2,1,0:T(8,128)(2,1)} %bitcast.33), calls=%async_computation.1 | async-start | bytes 4718592 | tf_op jit(solution)/shard_map/all_to_all | solution.py:338
  106.6 1.5 mix_weights.1.weights_ref
  108.1 55.1 %all-to-all-done.1 = bf16[128,8,1152]{2,1,0:T(8,128)(2,1)S(1)} async-done(((bf16[128,8,1152]{2,1,0:T(8,128)(2,1)}), bf16[128,8,1152]{2,1,0:T(8,128)(2,1)S(1)}, u32[]{:S(2)}, u32[]{:S(2)}) %all-to-all-start.1) | async-done | bytes 2359328 | tf_op jit(solution)/shard_map/all_to_all | solution.py:338
  163.2 1.8 %combine.1 = (bf16[2,64,1440]{2,1,0:T(8,128)(2,1)}, bf16[64,1440]{1,0:T(8,128)(2,1)S(1)}) custom-call(s32[1]{0:T(128)} %bitcast.h_ref, bf16[4,128,1024]{2,1,0:T(8,128)(2,1)S(1)} %mix_weights.1.weights_ref, bf16[1024,1152]{1,0:T(8,128)(2,1)S(1)} %bitcast.27), custom_call_target="tpu_custom_call" | custom-call | tf_op jit(solution)/shard_map/combine/pallas_call | solution.py:306
  165.0 4.4 %collective-permute-start.2 = (bf16[64,1440]{1,0:T(8,128)(2,1)S(1)}, bf16[64,1440]{1,0:T(8,128)(2,1)S(1)}, u32[]{:S(2)}, u32[]{:S(2)}) collective-permute-start(bf16[64,1440]{1,0:T(8,128)(2,1)S(1)} %get-tuple-element.12), channel_id=1, source_target_pairs={{0,1},{1,0},{2,3},{3,2},{4,5},{5,4},{6,7},{7,6},{8,9},{9,8},{10,11... | collective-permute-start | bytes 552968 | tf_op jit(solution)/shard_map/ppermute | solution.py:342
  169.3 1.1 collective-permute-done.2.other_ref
  170.4 0.7 finish.1
  (17 shorter events, 0.0 us)
Async XLA Ops:
  0.0 12.3 %slice-start = ((s8[4423680]{0:T(1024)(128)(4,1)}), s8[4194304]{0:T(1024)(128)(4,1)S(1)}, s32[]{:S(2)}) async-start(s8[4423680]{0:T(1024)(128)(4,1)} %bitcast.34), calls=%async_computation.2 | async-start | bytes 8388608
  3.9 7.7 %copy-start.7 = (bf16[1,90,768]{2,1,0:T(8,128)(2,1)S(1)}, bf16[1,90,768]{2,1,0:T(8,128)(2,1)}, u32[]{:S(2)}) copy-start(bf16[1,90,768]{2,1,0:T(8,128)(2,1)} %param.13) | copy-start | bytes 414724
  3.9 8.4 %slice-start.1 = ((s8[4423680]{0:T(1024)(128)(4,1)}), s8[229376]{0:T(1024)(128)(4,1)S(1)}, s32[]{:S(2)}) async-start(s8[4423680]{0:T(1024)(128)(4,1)} %bitcast.34), calls=%async_computation.3 | async-start | bytes 458752
  8.3 4.9 %copy-start.4 = (bf16[2880,768]{1,0:T(8,128)(2,1)}, bf16[2880,768]{1,0:T(8,128)(2,1)S(1)}, u32[]{:S(2)}) copy-start(bf16[2880,768]{1,0:T(8,128)(2,1)S(1)} %fusion.1.down_a_hbm) | copy-start | bytes 13271044
  8.3 74.7 %collective-permute-start.1 = (bf16[2880,768]{1,0:T(8,128)(2,1)S(1)}, bf16[2880,768]{1,0:T(8,128)(2,1)S(1)}, u32[]{:S(2)}, u32[]{:S(2)}) collective-permute-start(bf16[2880,768]{1,0:T(8,128)(2,1)S(1)} %fusion.1.down_a_hbm), channel_id=1, source_target_pairs={{0,1},{1,0},{2,3},{3,2},{4,5},{5,4},{6,7},{7,6},{8,9},{9,8},{10,11... | collective-permute-start | bytes 13271048 | tf_op jit(solution)/shard_map/ppermute | solution.py:342
  13.2 69.9 %copy-start.3 = (bf16[2880,768]{1,0:T(8,128)(2,1)}, bf16[2880,768]{1,0:T(8,128)(2,1)S(1)}, u32[]{:S(2)}) copy-start(bf16[2880,768]{1,0:T(8,128)(2,1)S(1)} %fusion.2.up_a_hbm) | copy-start | bytes 13271044
  13.2 69.8 %collective-permute-start = (bf16[2880,768]{1,0:T(8,128)(2,1)S(1)}, bf16[2880,768]{1,0:T(8,128)(2,1)S(1)}, u32[]{:S(2)}, u32[]{:S(2)}) collective-permute-start(bf16[2880,768]{1,0:T(8,128)(2,1)S(1)} %fusion.2.up_a_hbm), channel_id=1, source_target_pairs={{0,1},{1,0},{2,3},{3,2},{4,5},{5,4},{6,7},{7,6},{8,9},{9,8},{10,11... | collective-permute-start | bytes 13271048 | tf_op jit(solution)/shard_map/ppermute | solution.py:342
  83.0 2.0 %copy-start.5 = (bf16[2880,768]{1,0:T(8,128)(2,1)}, bf16[2880,768]{1,0:T(8,128)(2,1)S(1)}, u32[]{:S(2)}) copy-start(bf16[2880,768]{1,0:T(8,128)(2,1)S(1)} %collective-permute-done.1.down_b_hbm) | copy-start | bytes 13271044
  85.1 2.1 %copy-start.6 = (bf16[2880,768]{1,0:T(8,128)(2,1)}, bf16[2880,768]{1,0:T(8,128)(2,1)S(1)}, u32[]{:S(2)}) copy-start(bf16[2880,768]{1,0:T(8,128)(2,1)S(1)} %collective-permute-done.up_b_hbm) | copy-start | bytes 13271044
  100.2 6.4 %copy-start = (s32[2,64,4]{1,2,0:T(4,128)S(1)}, s32[2,64,4]{1,2,0:T(4,128)}, u32[]{:S(2)}) copy-start(s32[2,64,4]{1,2,0:T(4,128)} %param.9) | copy-start | bytes 6148
  100.2 6.4 %copy-start.1 = (f32[2,64,4]{1,2,0:T(4,128)S(1)}, f32[2,64,4]{1,2,0:T(4,128)}, u32[]{:S(2)}) copy-start(f32[2,64,4]{1,2,0:T(4,128)} %param.10) | copy-start | bytes 6148
  100.2 6.4 %copy-start.2 = (s32[32,2]{0,1:T(2,128)S(1)}, s32[32,2]{0,1:T(2,128)}, u32[]{:S(2)}) copy-start(s32[32,2]{0,1:T(2,128)} %param.11) | copy-start | bytes 772
  100.2 63.0 %all-to-all-start.1 = ((bf16[128,8,1152]{2,1,0:T(8,128)(2,1)}), bf16[128,8,1152]{2,1,0:T(8,128)(2,1)S(1)}, u32[]{:S(2)}, u32[]{:S(2)}) async-start(bf16[128,8,1152]{2,1,0:T(8,128)(2,1)} %bitcast.33), calls=%async_computation.1 | async-start | bytes 4718592 | tf_op jit(solution)/shard_map/all_to_all | solution.py:338
  165.0 5.4 %collective-permute-start.2 = (bf16[64,1440]{1,0:T(8,128)(2,1)S(1)}, bf16[64,1440]{1,0:T(8,128)(2,1)S(1)}, u32[]{:S(2)}, u32[]{:S(2)}) collective-permute-start(bf16[64,1440]{1,0:T(8,128)(2,1)S(1)} %get-tuple-element.12), channel_id=1, source_target_pairs={{0,1},{1,0},{2,3},{3,2},{4,5},{5,4},{6,7},{7,6},{8,9},{9,8},{10,11... | collective-permute-start | bytes 552968 | tf_op jit(solution)/shard_map/ppermute | solution.py:342
